TPU v7x, 32 devices: a whole 2x2x4 slice. The times are simulated.
32 devices in a mesh: gx: 8 (over y, x, core), gy: 4 (over z).
Axes of the slice: x: 2, y: 2, z: 4, core: 2. Of those that a mesh axis runs over, the one named last changes fastest.
Arguments:
- object_field: float32 [2, 8192, 4096], P(None, 'gx', 'gy'), may hold values from -5 to 5
- probe: float32 [2, 256, 256], replicated, may hold values from -5 to 5
- centers: int32 [512, 2], P(('gx', 'gy')), may hold values from 0 to 1023
- live: int32 [512], P(('gx', 'gy')), may hold values from 0 to 1, as said below
- measured: float32 [512, 256, 256], P(('gx', 'gy')), may hold values from 0.5 to 2.5
Outputs:
- object_grad: float32 [2, 8192, 4096], P(None, 'gx', 'gy')
- probe_grad: float32 [2, 256, 256], replicated
- slot_loss: float32 [512], P(('gx', 'gy'))
Inputs may be any that keep to these rules, and one draw needn't show every extreme that they name: In each tile's 16 slots the live ones come first; every tile has at least one live slot, and some tile has all 16 live.
All inputs are finite; a program needn't handle non-finite values.
Results may differ from a plain program's by a relative error of at most 0.0001.
Values sent between devices are 32-bit elements; how exact they have to be, the bound alone decides.
No kernel may reach another device: no remote copies, remote signals or barrier semaphores. Data moves between devices by JAX's collectives and lax.ppermute only.
A program may use at most 192 MiB of HBM per device.

v0:
```python
import functools
import math

import jax
import jax.numpy as jnp
import numpy as np
from jax import lax
from jax.experimental import pallas as pl
from jax.experimental.pallas import tpu as pltpu
from jax.sharding import PartitionSpec as P


LANES = 128
SUBS = 8
PLAN = "bfbfbfbfbfbfbfbfbfbfbfb"
BF = jnp.bfloat16
F32 = jnp.float32


def split_np(table):
    hi = table.astype(np.float32).astype(jnp.bfloat16)
    lo = (table - hi.astype(np.float64)).astype(np.float32).astype(jnp.bfloat16)
    return hi, lo


def tables_np(extent):
    half = extent // 2
    k = np.arange(extent)[:, None]
    n = np.arange(half)[None, :]
    angle = -2.0 * np.pi * ((k * n) % extent) / extent
    re = np.cos(angle) / math.sqrt(extent)
    im = np.sin(angle) / math.sqrt(extent)
    mats = []
    for parity in range(2):
        a, b = re[parity::2], im[parity::2]
        left = np.block([[a, -b], [b, a]])
        mats += [np.stack(split_np(left)), np.stack(split_np(left.T))]
    pick = np.zeros((extent, extent), np.float32)
    pick[2 * np.arange(half), np.arange(half)] = 1
    pick[2 * np.arange(half) + 1, half + np.arange(half)] = 1
    return np.stack(mats), pick.astype(jnp.bfloat16)


def parts(x):
    hi = x.astype(BF)
    lo = (x - hi.astype(F32)).astype(BF)
    return hi, lo


def matmul(a, b):
    return jnp.dot(a, b, preferred_element_type=F32)


def slot_kernel(
    phase, extent, slots, tile,
    centers, live, *refs,
):
    half = extent // 2
    inner = phase == "inner"
    it = iter(refs)
    take = lambda n: [next(it) for _ in range(n)]
    tile_hbm, probe, meas_hbm, mats, pick = take(5)
    if not inner:
        sides_hbm, corners_hbm = take(4), take(4)
        grad_in, acc_in, loss_in = take(3)
        del grad_in
    grad_out, acc_out, loss_out = take(3)
    if not inner:
        gsides, gcorners = take(4), take(4)
    ext, grad, shifted, accs, turned, kept, meas, sh_h, sh_l, z_h, z_l, sems, msems, order = take(14)
    mid = pl.ds(half, tile)
    low, high = pl.ds(0, half), pl.ds(half + tile, half)
    sides = ((low, mid), (high, mid), (mid, low), (mid, high))
    corners = ((low, low), (low, high), (high, low), (high, high))
    band = min(extent, tile // 2)
    rest = tile - 2 * band
    ring = [(0, band, 0, tile), (tile - band, band, 0, tile)]
    if rest:
        ring += [(band, rest, 0, band), (band, rest, tile - band, band)]

    copies = []

    def copy(src, dst):
        copies.append(pltpu.make_async_copy(src, dst, sems.at[len(copies)]))
        copies[-1].start()

    def own(ref, box, shift):
        return ref.at[:, pl.ds(box[0] + shift, box[1]), pl.ds(box[2] + shift, box[3])]

    def wanted(s):
        row = centers[s, 0]
        col = centers[s, 1]
        inside = (row >= half) & (row <= tile - half) & (col >= half) & (col <= tile - half)
        return (live[s] > 0) & (inside if inner else jnp.logical_not(inside))

    def fetch(s, j):
        return pltpu.make_async_copy(meas_hbm.at[s, :, pl.ds(j * LANES, LANES)], meas.at[j, s], msems.at[j, s])

    if inner:
        copy(tile_hbm, ext.at[:, mid, mid])
    else:
        for src, (rows, cols) in zip(sides_hbm + corners_hbm, sides + corners):
            copy(src, ext.at[:, rows, cols])
        for box in ring:
            copy(own(tile_hbm, box, 0), own(ext, box, half))
    loads = list(copies)

    def prefetch(s, n):
        go = wanted(s)
        order[n] = s

        @pl.when(go)
        def _():
            for j in range(2):
                fetch(s, j).start()

        return n + go.astype(jnp.int32)

    count = lax.fori_loop(0, slots, prefetch, jnp.int32(0))
    if not inner:
        for box in ring:
            copy(own(grad_out, box, 0), own(grad, box, half))
    late = copies[len(loads):]

    for p in range(2):
        plane = probe[p]
        for b in range(SUBS):
            shifted[b, p] = pltpu.roll(plane, b, 0) if b else plane
    accs[...] = jnp.zeros_like(accs)
    step_rows = 4 * SUBS

    def clear(rows, cols):
        block = jnp.zeros((2, step_rows, cols.size), F32)

        def body(i, c):
            at = pl.multiple_of(rows.start + i * step_rows, step_rows)
            grad[:, pl.ds(at, step_rows), cols] = block
            return c

        lax.fori_loop(0, rows.size // step_rows, body, 0)

    if inner:
        loss_out[...] = jnp.zeros_like(loss_out)
        clear(mid, mid)
    else:
        loss_out[...] = loss_in[...]
        for rows, cols in sides + corners:
            clear(rows, cols)
    for c in loads:
        c.wait()

    chunk = 32
    lane8 = lax.broadcasted_iota(jnp.int32, (SUBS, LANES), 1)
    sub8 = lax.broadcasted_iota(jnp.int32, (SUBS, LANES), 0)

    lane = lax.broadcasted_iota(jnp.int32, (chunk, LANES), 1)

    def place(s):
        row, col = centers[s, 0], centers[s, 1]
        b, r = lax.rem(row, SUBS), lax.rem(col, LANES)
        a8, q = row - b, col - r
        cols = [pl.ds(pl.multiple_of(q + j * LANES, LANES), LANES) for j in range(3)]
        at = lambda off: pl.ds(pl.multiple_of(a8 + off, SUBS), chunk)
        at8 = pl.ds(pl.multiple_of(a8 + extent, SUBS), SUBS)
        return b, r, cols, at, at8

    def patch(where, p, i):
        b, r, cols, at, at8 = where
        c0 = jnp.where(lane >= r, ext[p, at(i), cols[0]], ext[p, at(i), cols[2]])
        c1 = ext[p, at(i), cols[1]]
        if i == 0:
            x0 = jnp.where(lane8 >= r, ext[p, at8, cols[0]], ext[p, at8, cols[2]])
            x1 = ext[p, at8, cols[1]]
            c0 = jnp.concatenate([jnp.where(sub8 >= b, c0[:SUBS], x0), c0[SUBS:]], axis=0)
            c1 = jnp.concatenate([jnp.where(sub8 >= b, c1[:SUBS], x1), c1[SUBS:]], axis=0)
        return c0, c1

    def left_mul(m, hi, lo):
        table = jnp.concatenate([mats[m, 0], mats[m, 1], mats[m, 0]], axis=1)
        return matmul(table, jnp.concatenate([hi, hi, lo], axis=0))

    def right_mul(hi, lo, m):
        table = jnp.concatenate([mats[m, 0], mats[m, 1], mats[m, 0]], axis=0)
        return matmul(jnp.concatenate([hi, hi, lo], axis=1), table)

    def front(s):
        where = place(s)
        b, r = where[:2]

        def turn(p, i):
            r0 = pltpu.roll(shifted[b, p, i:i + chunk, :LANES], r, 1)
            r1 = pltpu.roll(shifted[b, p, i:i + chunk, LANES:], r, 1)
            return jnp.where(lane >= r, r0, r1), jnp.where(lane >= r, r1, r0)

        def wave(i):
            o_re, o_im = patch(where, 0, i), patch(where, 1, i)
            p_re, p_im = turn(0, i), turn(1, i)
            out = []
            for j in range(2):
                js = slice(j * LANES, (j + 1) * LANES)
                turned[0, i:i + chunk, js] = p_re[j]
                turned[1, i:i + chunk, js] = p_im[j]
                out.append((p_re[j] * o_re[j] - p_im[j] * o_im[j], p_re[j] * o_im[j] + p_im[j] * o_re[j]))
            return out

        for i in range(0, half, chunk):
            top, bot = wave(i), wave(i + half)
            for j in range(2):
                js = slice(j * LANES, (j + 1) * LANES)
                for c in range(2):
                    for e, v in enumerate((top[j][c] + bot[j][c], top[j][c] - bot[j][c])):
                        hi, lo = parts(v)
                        sh_h[e, c * half + i:c * half + i + chunk, js] = hi
                        sh_l[e, c * half + i:c * half + i + chunk, js] = lo
            yield
        mids = []
        for e in range(2):
            y = left_mul(2 * e, sh_h[e], sh_l[e])
            mids.append((y[:half], y[half:]))
            yield
        far = []
        for e in range(2):
            rows = []
            for re, im in mids:
                if e == 0:
                    halves = [re[:, :half] + re[:, half:], im[:, :half] + im[:, half:]]
                else:
                    halves = [re[:, :half] - re[:, half:], im[:, :half] - im[:, half:]]
                rows.append(jnp.concatenate(halves, axis=1))
            hi, lo = parts(jnp.concatenate(rows, axis=0))
            far.append(right_mul(hi, lo, 2 * e + 1))
            yield
        m_rows = jnp.concatenate(
            [
                jnp.concatenate([meas[j, s, pl.ds(e, half, stride=2), :] for j in range(2)], axis=1)
                for e in range(2)
            ],
            axis=0,
        )
        m_hi, m_lo = parts(m_rows)
        amp = matmul(jnp.concatenate([m_hi, m_lo], axis=1), jnp.concatenate([pick[...]] * 2, axis=0))
        yield
        total = jnp.zeros((SUBS, LANES), F32)
        for e in range(2):
            re, im = far[e][:, :half], far[e][:, half:]
            t = re * re + im * im + 1.0
            inv = lax.rsqrt(t)
            differ = t * inv - amp[:, e * half:(e + 1) * half]
            total = total + jnp.sum((differ * differ).reshape(extent // SUBS, SUBS, half), axis=0)
            factor = differ * inv
            hi, lo = parts(jnp.concatenate([re * factor, im * factor], axis=1))
            z_h[e] = hi
            z_l[e] = lo
            yield
        loss_out[s] = total

    def back(s):
        where = place(s)
        b, r, cols, at, at8 = where
        backs = []
        for e in range(2):
            backs.append(right_mul(z_h[e], z_l[e], 2 * e))
            yield
        outs = []
        for e in range(2):
            rs = slice(e * half, (e + 1) * half)
            left, right = backs[0][rs] + backs[1][rs], backs[0][rs] - backs[1][rs]
            x = jnp.concatenate(
                [
                    jnp.concatenate([left[:, :half], right[:, :half]], axis=1),
                    jnp.concatenate([left[:, half:], right[:, half:]], axis=1),
                ],
                axis=0,
            )
            hi, lo = parts(x)
            outs.append(left_mul(2 * e + 1, hi, lo))
            yield
        for k in range(2):
            for i0 in range(0, half, chunk):
                i = k * half + i0
                o_re, o_im = patch(where, 0, i), patch(where, 1, i)
                q_re, q_im = [], []
                for j in range(2):
                    js = slice(j * LANES, (j + 1) * LANES)
                    pair = [(outs[0][at0:at0 + chunk, js], outs[1][at0:at0 + chunk, js]) for at0 in (i0, half + i0)]
                    b_re, b_im = [(u + v) if k == 0 else (u - v) for u, v in pair]
                    p_re, p_im = kept[0, i:i + chunk, js], kept[1, i:i + chunk, js]
                    g_re = p_re * b_re + p_im * b_im
                    g_im = p_re * b_im - p_im * b_re
                    q_re.append(o_re[j] * b_re + o_im[j] * b_im)
                    q_im.append(o_re[j] * b_im - o_im[j] * b_re)
                    for p, g in enumerate((g_re, g_im)):
                        if i == 0:
                            spill = jnp.where(sub8 < b, g[:SUBS], 0.0)
                            g = jnp.concatenate([jnp.where(sub8 >= b, g[:SUBS], 0.0), g[SUBS:]], axis=0)
                        if j == 0:
                            grad[p, at(i), cols[0]] += jnp.where(lane >= r, g, 0.0)
                            grad[p, at(i), cols[2]] += jnp.where(lane < r, g, 0.0)
                            if i == 0:
                                grad[p, at8, cols[0]] += jnp.where(lane8 >= r, spill, 0.0)
                                grad[p, at8, cols[2]] += jnp.where(lane8 < r, spill, 0.0)
                        else:
                            grad[p, at(i), cols[1]] += g
                            if i == 0:
                                grad[p, at8, cols[1]] += spill
                turn_back = lax.rem(LANES - r, LANES)
                for p, (h0, h1) in enumerate((q_re, q_im)):
                    h0 = pltpu.roll(h0, turn_back, 1)
                    h1 = pltpu.roll(h1, turn_back, 1)
                    keep = lane < LANES - r
                    accs[b, p, i:i + chunk, :LANES] += jnp.where(keep, h0, h1)
                    accs[b, p, i:i + chunk, LANES:] += jnp.where(keep, h1, h0)
                yield

    def run(streams, plan=""):
        left = dict(streams)
        for name in plan:
            next(left[name])
        for stream in left.values():
            for _ in stream:
                pass

    def keep_probe():
        for p in range(2):
            kept[p] = turned[p]

    def ready(s):
        for j in range(2):
            fetch(s, j).wait()

    @pl.when(count > 0)
    def _():
        ready(order[0])
        run({"f": front(order[0])})
        keep_probe()

    for c in late:
        c.wait()

    def step(t, c):
        ready(order[t])
        run({"b": back(order[t - 1]), "f": front(order[t])}, PLAN)
        keep_probe()
        return c

    lax.fori_loop(1, count, step, 0)

    @pl.when(count > 0)
    def _():
        run({"b": back(order[count - 1])})

    copies.clear()
    if inner:
        copy(grad.at[:, mid, mid], grad_out)
    else:
        for dst, (rows, cols) in zip(gsides + gcorners, sides + corners):
            copy(grad.at[:, rows, cols], dst)
        for box in ring:
            copy(own(grad, box, half), own(grad_out, box, 0))
    for p in range(2):
        acc = accs[0, p]
        for b in range(1, SUBS):
            acc = acc + pltpu.roll(accs[b, p], extent - b, 0)
        for j in range(extent // LANES):
            at = pl.ds((p * (extent // LANES) + j) * extent, extent)
            part = acc[:, j * LANES:(j + 1) * LANES]
            acc_out[at, :] = part if inner else part + acc_in[at, :]
    for c in copies:
        c.wait()


def run_slots(phase, centers, live, tile_obj, probe, measured, tables, extra=()):
    extent = probe.shape[1]
    half = extent // 2
    slots = centers.shape[0]
    tile = tile_obj.shape[1]
    size = tile + 2 * half
    inner = phase == "inner"
    smem = pl.BlockSpec(memory_space=pltpu.SMEM)
    hbm = pl.BlockSpec(memory_space=pl.ANY)
    vmem = pl.BlockSpec(memory_space=pltpu.VMEM)
    in_specs = [smem, smem, hbm, vmem, hbm, vmem, vmem]
    out_shape = [
        jax.ShapeDtypeStruct((2, tile, tile), F32),
        jax.ShapeDtypeStruct((2 * extent * extent // LANES, LANES), F32),
        jax.ShapeDtypeStruct((slots, SUBS, LANES), F32),
    ]
    out_specs = [hbm, vmem, vmem]
    if not inner:
        in_specs += [hbm] * 9 + [vmem, vmem]
        out_shape += [jax.ShapeDtypeStruct((2, half, tile), F32)] * 2
        out_shape += [jax.ShapeDtypeStruct((2, tile, half), F32)] * 2
        out_shape += [jax.ShapeDtypeStruct((2, half, half), F32)] * 4
        out_specs += [hbm] * 8
    flops = slots * 16 * 2 * extent**3
    return pl.pallas_call(
        functools.partial(slot_kernel, phase, extent, slots, tile),
        out_shape=out_shape,
        in_specs=in_specs,
        out_specs=out_specs,
        scratch_shapes=[
            pltpu.VMEM((2, size, size), F32),
            pltpu.VMEM((2, size, size), F32),
            pltpu.VMEM((SUBS, 2, extent, extent), F32),
            pltpu.VMEM((SUBS, 2, extent, extent), F32),
            pltpu.VMEM((2, extent, extent), F32),
            pltpu.VMEM((2, extent, extent), F32),
            pltpu.VMEM((2, slots, extent, LANES), F32),
            pltpu.VMEM((2, extent, extent), BF),
            pltpu.VMEM((2, extent, extent), BF),
            pltpu.VMEM((2, extent, extent), BF),
            pltpu.VMEM((2, extent, extent), BF),
            pltpu.SemaphoreType.DMA((16,)),
            pltpu.SemaphoreType.DMA((2, slots)),
            pltpu.SMEM((slots + 1,), jnp.int32),
        ],
        compiler_params=pltpu.CompilerParams(vmem_limit_bytes=60 * 2**20),
        cost_estimate=pl.CostEstimate(flops=flops, bytes_accessed=32 * 2**20, transcendentals=0),
        input_output_aliases={} if inner else {len(in_specs) - 3: 0},
    )(centers, live, tile_obj, probe, measured, *tables, *extra)


def sum_all(x, groups, scale, shape):
    flat = x

    def send(y, axis, stride, count, k):
        n = lax.axis_size(axis)
        spot = lambda i: (i // stride) % count
        pairs = [(i, i + ((spot(i) + k) % count - spot(i)) * stride) for i in range(n)]
        return lax.ppermute(y, axis, pairs)

    def place(axis, stride, count):
        return lax.rem(lax.axis_index(axis) // stride, count)

    for axis, stride, count in groups:
        me = place(axis, stride, count)
        rows = flat.shape[0] // count
        own = lax.dynamic_slice_in_dim(flat, me * rows, rows, 0)
        got = [
            send(lax.dynamic_slice_in_dim(flat, lax.rem(me + k, count) * rows, rows, 0), axis, stride, count, k)
            for k in range(1, count)
        ]
        flat = sum(got, own)
    for level, (axis, stride, count) in reversed(list(enumerate(groups))):
        pieces = [flat] + [send(flat, axis, stride, count, k) for k in range(1, count)]
        me = place(axis, stride, count)
        if level == 0 and count == 2:
            return finish(me, pieces, scale, shape)
        rows = flat.shape[0]
        out = jnp.zeros((count * rows, LANES), F32)
        for k, piece in enumerate(pieces):
            out = lax.dynamic_update_slice_in_dim(out, piece, lax.rem(me + count - k, count) * rows, 0)
        flat = out
    return finish(jnp.int32(0), [flat], scale, shape)


def finish_kernel(scale, me, *refs):
    pieces, out = refs[:-1], refs[-1]
    planes, extent, width = out.shape
    each = planes // len(pieces)
    for k, piece in enumerate(pieces):
        owner = me[0] if k == 0 else len(pieces) - 1 - me[0]
        for p in range(each):
            for j in range(width // LANES):
                at = (p * (width // LANES) + j) * extent
                out[owner * each + p, :, j * LANES:(j + 1) * LANES] = piece[at:at + extent, :] * scale


def finish(me, pieces, scale, shape):
    vmem = pl.BlockSpec(memory_space=pltpu.VMEM)
    return pl.pallas_call(
        functools.partial(finish_kernel, scale),
        out_shape=jax.ShapeDtypeStruct(shape, F32),
        in_specs=[pl.BlockSpec(memory_space=pltpu.SMEM)] + [vmem] * len(pieces),
        out_specs=vmem,
        compiler_params=pltpu.CompilerParams(vmem_limit_bytes=8 * 2**20),
        cost_estimate=pl.CostEstimate(flops=2**17, bytes_accessed=2**20, transcendentals=0),
        name="finish",
    )(me.reshape(1), *pieces)


def sum_groups():
    nx, ny = lax.axis_size("gx"), lax.axis_size("gy")
    groups = [("gx", 1, 2), ("gx", 2, nx // 2)] if nx % 2 == 0 else [("gx", 1, nx)]
    return [g for g in groups + [("gy", 1, ny)] if g[2] > 1]


def fold_kernel(half, tile, main, *refs):
    adds, corners = refs[:4], refs[4:8]
    out, rows_buf, cols_buf, rows_add, cols_add, corner_add, sems = refs[8:]
    del main
    inside = tile - 2 * half
    copies = []

    def copy(src, dst):
        copies.append(pltpu.make_async_copy(src, dst, sems.at[len(copies)]))
        copies[-1].start()

    far = tile - half
    rows_at = [out.at[:, pl.ds(r, half), :] for r in (0, far)]
    cols_at = [out.at[:, pl.ds(half, inside), pl.ds(c, half)] for c in (0, far)]
    for k in range(2):
        copy(rows_at[k], rows_buf.at[k])
        copy(adds[k], rows_add.at[k])
        copy(cols_at[k], cols_buf.at[k])
        copy(adds[2 + k], cols_add.at[k])
    for k in range(4):
        copy(corners[k], corner_add.at[k])
    for c in copies:
        c.wait()
    copies.clear()
    step = 4 * SUBS
    for k in range(2):
        def rows_body(i, c, k=k):
            at = pl.ds(pl.multiple_of(i * step, step), step)
            side_at = pl.ds(pl.multiple_of(i * step + k * far, step), step)
            for p in range(2):
                rows_buf[k, p, at, :] += rows_add[k, p, at, :]
                for j, c0 in enumerate((0, far)):
                    lanes = slice(c0, c0 + half)
                    rows_buf[k, p, at, lanes] += cols_add[j, p, side_at, :] + corner_add[2 * k + j, p, at, :]
            return c

        lax.fori_loop(0, half // step, rows_body, 0)
        copy(rows_buf.at[k], rows_at[k])

        def cols_body(i, c, k=k):
            at = pl.ds(pl.multiple_of(i * step, step), step)
            side_at = pl.ds(pl.multiple_of(half + i * step, step), step)
            for p in range(2):
                cols_buf[k, p, at, :] += cols_add[k, p, side_at, :]
            return c

        lax.fori_loop(0, inside // step, cols_body, 0)
        copy(cols_buf.at[k], cols_at[k])
    for c in copies:
        c.wait()


def fold(main, adds, corners):
    tile = main.shape[1]
    half = adds[0].shape[1]
    hbm = pl.BlockSpec(memory_space=pl.ANY)
    return pl.pallas_call(
        functools.partial(fold_kernel, half, tile),
        out_shape=jax.ShapeDtypeStruct(main.shape, F32),
        in_specs=[hbm] * 9,
        out_specs=hbm,
        scratch_shapes=[
            pltpu.VMEM((2, 2, half, tile), F32),
            pltpu.VMEM((2, 2, tile - 2 * half, half), F32),
            pltpu.VMEM((2, 2, half, tile), F32),
            pltpu.VMEM((2, 2, tile, half), F32),
            pltpu.VMEM((4, 2, half, half), F32),
            pltpu.SemaphoreType.DMA((12,)),
        ],
        input_output_aliases={0: 0},
        compiler_params=pltpu.CompilerParams(vmem_limit_bytes=24 * 2**20),
        cost_estimate=pl.CostEstimate(flops=2**21, bytes_accessed=14 * 2**20, transcendentals=0),
        name="fold",
    )(main, *adds, *corners)


def shift2(x, dx, dy):
    nx, ny = lax.axis_size("gx"), lax.axis_size("gy")
    pairs = [
        (i * ny + j, (i + dx) * ny + j + dy)
        for i in range(nx)
        for j in range(ny)
        if 0 <= i + dx < nx and 0 <= j + dy < ny
    ]
    return lax.ppermute(x, ("gx", "gy"), pairs)


SIDES = ((1, 0), (-1, 0), (0, 1), (0, -1))
CORNERS = ((1, 1), (1, -1), (-1, 1), (-1, -1))


def on_device(object_field, probe, centers, live, measured):
    extent = probe.shape[1]
    half = extent // 2
    tile = object_field.shape[1]
    slots = centers.shape[0]
    tables = [jnp.asarray(t) for t in tables_np(extent)]
    far = tile - half

    def end(step):
        if step == 0:
            return slice(None)
        return slice(far, tile) if step == 1 else slice(0, half)

    def bring(dx, dy):
        return shift2(object_field[:, end(dx), end(dy)], dx, dy)

    left, right = bring(0, 1), bring(0, -1)
    up, down = bring(1, 0), bring(-1, 0)

    corners = [bring(dx, dy) for dx, dy in CORNERS]
    grad_a, acc_a, loss_a = run_slots("inner", centers, live, object_field, probe, measured, tables)
    out = run_slots(
        "outer", centers, live, object_field, probe, measured, tables,
        (up, down, left, right, *corners, grad_a, acc_a, loss_a),
    )
    grad_b, acc_b, loss_b = out[:3]
    sent = {}
    for places in ((2, 3), (0, 1), (4, 5, 6, 7)):
        for k in places:
            dx, dy = (SIDES + CORNERS)[k]
            sent[k] = shift2(out[3 + k], -dx, -dy)
    sides = [sent[1], sent[0], sent[3], sent[2]]
    corners = [sent[7], sent[6], sent[5], sent[4]]
    slots_all = slots * lax.axis_size("gx") * lax.axis_size("gy")
    probe_grad = sum_all(acc_b, sum_groups(), 1.0 / math.sqrt(slots_all), probe.shape)
    object_grad = fold(grad_b, sides, corners)

    slot_loss = jnp.sum(loss_b, axis=(1, 2)) * (0.5 / (extent * extent))
    return object_grad, probe_grad, slot_loss


def solution(mesh):
    placed = (
        P(None, "gx", "gy"),
        P(),
        P(("gx", "gy"), None),
        P(("gx", "gy")),
        P(("gx", "gy"), None, None),
    )
    return jax.shard_map(
        on_device,
        mesh=mesh,
        in_specs=placed,
        out_specs=(P(None, "gx", "gy"), P(), P(("gx", "gy"))),
        check_vma=False,
    )
```

profile of v0, /device:TPU:0, one launch (start us, length us, event | category | flops | bytes accessed | tf_op | source)
XLA Modules:
  0.0 185.7 jit_solution(5524722982658401158)
XLA Ops:
  0.6 1.7 fusion.2
  2.3 3.4 %collective-permute-start = (f32[2,128,1024]{2,1,0:T(8,128)S(1)}, f32[2,128,1024]{2,1,0:T(8,128)}, u32[]{:S(2)}, u32[]{:S(2)}) collective-permute-start(f32[2,128,1024]{2,1,0:T(8,128)S(1)} %get-tuple-element.40), channel_id=1, source_target_pairs={{0,4},{1,5},{2,6},{3,7},{4,8},{5,9},{6,10},{7,11},{8,12},{9,13},{1... | collective-permute-start | bytes 3145736 | tf_op jit(solution)/shard_map/ppermute | solution.py:572
  5.7 1.3 collective-permute-start.1
  7.0 1.1 fusion
  8.2 5.3 %collective-permute-start.4 = (f32[2,128,128]{2,1,0:T(8,128)S(1)}, f32[2,128,128]{2,1,0:T(8,128)S(1)}, u32[]{:S(2)}, u32[]{:S(2)}) collective-permute-start(f32[2,128,128]{2,1,0:T(8,128)S(1)} %get-tuple-element.36), channel_id=1, source_target_pairs={{0,5},{1,6},{2,7},{4,9},{5,10},{6,11},{8,13},{9,14},{10,15},{12,17... | collective-permute-start | bytes 393224 | tf_op jit(solution)/shard_map/ppermute | solution.py:572
  14.2 2.7 %fusion.1 = (f32[2,1024,128]{2,1,0:T(8,128)S(1)}, f32[2,1024,128]{2,1,0:T(8,128)}) fusion(f32[2,1024,1024]{2,1,0:T(8,128)} %refs_0_.3), kind=kLoop, calls=%fused_computation.20 | loop fusion | bytes 4194304 | tf_op jit(solution)/shard_map/slice | solution.py:593
  16.9 7.3 %collective-permute-start.2 = (f32[2,1024,128]{2,1,0:T(8,128)}, f32[2,1024,128]{2,1,0:T(8,128)}, u32[]{:S(2)}, u32[]{:S(2)}) collective-permute-start(f32[2,1024,128]{2,1,0:T(8,128)} %get-tuple-element.38), channel_id=1, source_target_pairs={{0,1},{1,2},{2,3},{4,5},{5,6},{6,7},{8,9},{9,10},{10,11},{12,13},{... | collective-permute-start | bytes 3145736 | tf_op jit(solution)/shard_map/ppermute | solution.py:572
  24.2 1.3 collective-permute-start.3
  26.2 1.3 collective-permute-start.6
  28.2 1.3 collective-permute-start.7
  29.4 20.3 %shard_map.94 = (f32[2,1024,1024]{2,1,0:T(8,128)}, f32[1024,128]{1,0:T(8,128)}, f32[16,8,128]{2,1,0:T(8,128)}) custom-call(s32[16,2]{1,0:T(8,128)} %copy.13.centers, s32[16]{0:T(128)} %live.3, f32[2,1024,1024]{2,1,0:T(8,128)} %refs_0_.3, f32[2,256,256]{2,1,0:T(8,128)} %refs_1_.3, f32[16,256,256]{2,1,0:T(8,128)} %refs_2_.3, ...), custom_call_target="tpu_custom_call" | custom-call | flops 8589934592 | bytes 33554432 | tf_op jit(solution)/shard_map/pallas_call | solution.py:396
  49.7 7.4 %collective-permute-done.7.refs_12_ = f32[2,128,128]{2,1,0:T(8,128)S(1)} collective-permute-done((f32[2,128,128]{2,1,0:T(8,128)S(1)}, f32[2,128,128]{2,1,0:T(8,128)S(1)}, u32[]{:S(2)}, u32[]{:S(2)}) %collective-permute-start.7) | collective-permute-done | bytes 131104 | tf_op jit(solution)/shard_map/ppermute | solution.py:572
  57.8 17.7 %shard_map.95 = (f32[2,1024,1024]{2,1,0:T(8,128)}, f32[1024,128]{1,0:T(8,128)}, f32[16,8,128]{2,1,0:T(8,128)}, f32[2,128,1024]{2,1,0:T(8,128)}, f32[2,128,1024]{...) custom-call(s32[16,2]{1,0:T(8,128)} %copy.13.centers, ...), custom_call_target="tpu_custom_call", output_to_operand_aliasing={{0}: (15, {})} | custom-call | flops 8589934592 | bytes 33554432 | tf_op jit(solution)/shard_map/pallas_call | solution.py:396
  75.5 1.0 constant_dynamic-slice_fusion.6
  76.4 24.1 %collective-permute-start.16 = (f32[512,128]{1,0:T(8,128)S(1)}, f32[512,128]{1,0:T(8,128)S(1)}, u32[]{:S(2)}, u32[]{:S(2)}) collective-permute-start(f32[512,128]{1,0:T(8,128)S(1)} %constant_dynamic-slice_fusion.6), channel_id=1, source_target_pairs={{0,4},{4,0},{8,12},{12,8},{16,20},{20,16},{24,28},{28,24},{1,5},{5... | collective-permute-start | bytes 786440 | tf_op jit(solution)/shard_map/ppermute | solution.py:430
  100.6 1.2 collective-permute-done.16
  101.7 1.0 dynamic-slice_add_fusion
  102.9 1.9 %collective-permute-start.17 = (f32[128,128]{1,0:T(8,128)S(1)}, f32[128,128]{1,0:T(8,128)S(1)}, u32[]{:S(2)}, u32[]{:S(2)}) collective-permute-start(f32[128,128]{1,0:T(8,128)S(1)} %get-tuple-element.41), channel_id=1, source_target_pairs={{0,8},{4,12},{8,16},{12,20},{16,24},{20,28},{24,0},{28,4},{1,9},{5... | collective-permute-start | bytes 196616 | tf_op jit(solution)/shard_map/ppermute | solution.py:430
  104.8 2.5 %collective-permute-done.19 = f32[128,128]{1,0:T(8,128)S(1)} collective-permute-done((f32[128,128]{1,0:T(8,128)S(1)}, f32[128,128]{1,0:T(8,128)S(1)}, u32[]{:S(2)}, u32[]{:S(2)}) %collective-permute-start.19) | collective-permute-done | bytes 65568 | tf_op jit(solution)/shard_map/ppermute | solution.py:430
  107.3 1.3 collective-permute-done.18
  108.7 2.6 %collective-permute-start.22 = (f32[32,128]{1,0:T(8,128)S(1)}, f32[32,128]{1,0:T(8,128)S(1)}, u32[]{:S(2)}, u32[]{:S(2)}) collective-permute-start(f32[32,128]{1,0:T(8,128)S(1)} %get-tuple-element.45), channel_id=1, source_target_pairs={{0,3},{1,0},{2,1},{3,2},{4,7},{5,4},{6,5},{7,6},{8,11},{9,8},{10,9... | collective-permute-start | bytes 49160 | tf_op jit(solution)/shard_map/ppermute | solution.py:430
  111.3 4.1 %collective-permute-start.21 = (f32[32,128]{1,0:T(8,128)S(1)}, f32[32,128]{1,0:T(8,128)S(1)}, u32[]{:S(2)}, u32[]{:S(2)}) collective-permute-start(f32[32,128]{1,0:T(8,128)S(1)} %get-tuple-element.46), channel_id=1, source_target_pairs={{0,2},{1,3},{2,0},{3,1},{4,6},{5,7},{6,4},{7,5},{8,10},{9,11},{10,... | collective-permute-start | bytes 49160 | tf_op jit(solution)/shard_map/ppermute | solution.py:430
  115.5 1.9 %collective-permute-start.20 = (f32[32,128]{1,0:T(8,128)S(1)}, f32[32,128]{1,0:T(8,128)S(1)}, u32[]{:S(2)}, u32[]{:S(2)}) collective-permute-start(f32[32,128]{1,0:T(8,128)S(1)} %get-tuple-element.44), channel_id=1, source_target_pairs={{0,1},{1,2},{2,3},{3,0},{4,5},{5,6},{6,7},{7,4},{8,9},{9,10},{10,1... | collective-permute-start | bytes 49160 | tf_op jit(solution)/shard_map/ppermute | solution.py:430
  117.4 3.6 %collective-permute-done.20 = f32[32,128]{1,0:T(8,128)S(1)} collective-permute-done((f32[32,128]{1,0:T(8,128)S(1)}, f32[32,128]{1,0:T(8,128)S(1)}, u32[]{:S(2)}, u32[]{:S(2)}) %collective-permute-start.20) | collective-permute-done | bytes 16416 | tf_op jit(solution)/shard_map/ppermute | solution.py:430
  122.4 1.3 collective-permute-start.8
  123.8 1.3 collective-permute-start.9
  125.1 2.8 %collective-permute-start.12 = (f32[2,128,128]{2,1,0:T(8,128)}, f32[2,128,128]{2,1,0:T(8,128)S(1)}, u32[]{:S(2)}, u32[]{:S(2)}) collective-permute-start(f32[2,128,128]{2,1,0:T(8,128)} %get-tuple-element.25), channel_id=1, source_target_pairs={{0,5},{1,6},{2,7},{4,9},{5,10},{6,11},{8,13},{9,14},{10,15},{12,17... | collective-permute-start | bytes 393224 | tf_op jit(solution)/shard_map/ppermute | solution.py:572
  128.6 5.2 %collective-permute-start.24 = (f32[32,128]{1,0:T(8,128)S(1)}, f32[32,128]{1,0:T(8,128)S(1)}, u32[]{:S(2)}, u32[]{:S(2)}) collective-permute-start(f32[32,128]{1,0:T(8,128)S(1)} %get-tuple-element.32), channel_id=1, source_target_pairs={{0,2},{1,3},{2,0},{3,1},{4,6},{5,7},{6,4},{7,5},{8,10},{9,11},{10,... | collective-permute-start | bytes 49160 | tf_op jit(solution)/shard_map/ppermute | solution.py:430
  134.4 3.2 %collective-permute-done.24 = f32[32,128]{1,0:T(8,128)S(1)} collective-permute-done((f32[32,128]{1,0:T(8,128)S(1)}, f32[32,128]{1,0:T(8,128)S(1)}, u32[]{:S(2)}, u32[]{:S(2)}) %collective-permute-start.24) | collective-permute-done | bytes 16416 | tf_op jit(solution)/shard_map/ppermute | solution.py:430
  137.6 3.6 %collective-permute-start.25 = (f32[32,128]{1,0:T(8,128)S(1)}, f32[32,128]{1,0:T(8,128)S(1)}, u32[]{:S(2)}, u32[]{:S(2)}) collective-permute-start(f32[32,128]{1,0:T(8,128)S(1)} %get-tuple-element.32), channel_id=1, source_target_pairs={{0,3},{1,0},{2,1},{3,2},{4,7},{5,4},{6,5},{7,6},{8,11},{9,8},{10,9... | collective-permute-start | bytes 49160 | tf_op jit(solution)/shard_map/ppermute | solution.py:430
  141.8 2.0 %collective-permute-start.10 = (f32[2,1024,128]{2,1,0:T(8,128)}, f32[2,1024,128]{2,1,0:T(8,128)S(1)}, u32[]{:S(2)}, u32[]{:S(2)}) collective-permute-start(f32[2,1024,128]{2,1,0:T(8,128)} %get-tuple-element.23), channel_id=1, source_target_pairs={{0,1},{1,2},{2,3},{4,5},{5,6},{6,7},{8,9},{9,10},{10,11},{12,13},{... | collective-permute-start | bytes 3145736 | tf_op jit(solution)/shard_map/ppermute | solution.py:572
  143.8 1.3 collective-permute-start.11
  146.4 3.3 %collective-permute-start.26 = (f32[128,128]{1,0:T(8,128)}, f32[128,128]{1,0:T(8,128)S(1)}, u32[]{:S(2)}, u32[]{:S(2)}) collective-permute-start(f32[128,128]{1,0:T(8,128)} %constant_dynamic-update-slice_fusion.4), channel_id=1, source_target_pairs={{0,8},{4,12},{8,16},{12,20},{16,24},{20,28},{24,0},{28,4},{1,9},{5... | collective-permute-start | bytes 196616 | tf_op jit(solution)/shard_map/ppermute | solution.py:430
  149.7 2.2 %collective-permute-done.26 = f32[128,128]{1,0:T(8,128)S(1)} collective-permute-done((f32[128,128]{1,0:T(8,128)}, f32[128,128]{1,0:T(8,128)S(1)}, u32[]{:S(2)}, u32[]{:S(2)}) %collective-permute-start.26) | collective-permute-done | bytes 65568 | tf_op jit(solution)/shard_map/ppermute | solution.py:430
  152.5 3.0 %collective-permute-start.27 = (f32[128,128]{1,0:T(8,128)}, f32[128,128]{1,0:T(8,128)S(1)}, u32[]{:S(2)}, u32[]{:S(2)}) collective-permute-start(f32[128,128]{1,0:T(8,128)} %constant_dynamic-update-slice_fusion.4), channel_id=1, source_target_pairs={{0,16},{4,20},{8,24},{12,28},{16,0},{20,4},{24,8},{28,12},{1,17},{... | collective-permute-start | bytes 196616 | tf_op jit(solution)/shard_map/ppermute | solution.py:430
  155.6 0.9 constant_dynamic-update-slice_fusion.3
  156.4 1.6 collective-permute-done.27
  158.0 0.7 collective-permute-start.28
  158.7 0.8 constant_dynamic-update-slice_fusion.2
  159.5 2.9 %collective-permute-done.28 = f32[128,128]{1,0:T(8,128)S(1)} collective-permute-done((f32[128,128]{1,0:T(8,128)}, f32[128,128]{1,0:T(8,128)S(1)}, u32[]{:S(2)}, u32[]{:S(2)}) %collective-permute-start.28) | collective-permute-done | bytes 65568 | tf_op jit(solution)/shard_map/ppermute | solution.py:430
  163.8 5.5 %collective-permute-start.29 = (f32[512,128]{1,0:T(8,128)S(1)}, f32[512,128]{1,0:T(8,128)}, u32[]{:S(2)}, u32[]{:S(2)}) collective-permute-start(f32[512,128]{1,0:T(8,128)S(1)} %constant_dynamic-update-slice_fusion.refs_0_), channel_id=1, source_target_pairs={{0,4},{4,0},{8,12},{12,8},{16,20},{20,16},{24,28},{28,24},{1,5},{5... | collective-permute-start | bytes 786440 | tf_op jit(solution)/shard_map/ppermute | solution.py:430
  169.3 1.0 reduce_sum.9
  170.6 1.3 collective-permute-start.15
  172.4 1.8 finish.1
  174.2 5.1 %collective-permute-done.15.refs_7_ = f32[2,128,128]{2,1,0:T(8,128)S(1)} collective-permute-done((f32[2,128,128]{2,1,0:T(8,128)}, f32[2,128,128]{2,1,0:T(8,128)S(1)}, u32[]{:S(2)}, u32[]{:S(2)}) %collective-permute-start.15) | collective-permute-done | bytes 131104 | tf_op jit(solution)/shard_map/ppermute | solution.py:572
  179.4 0.9 copy-done.1
  180.3 0.9 copy-done.3
  181.2 4.5 %fold.1 = f32[2,1024,1024]{2,1,0:T(8,128)} custom-call(f32[2,1024,1024]{2,1,0:T(8,128)} %get-tuple-element.20.main, f32[2,128,1024]{2,1,0:T(8,128)S(1)} %collective-permute-done.8.refs_0_, f32[2,128,1024]{2,1,0:T(8,128)S(1)} %collective-permute-done.9.refs_1_, f32[2,1024,128]{2,1,0:T(8,128)S(1)} %collective-permute-done.10.refs_2_, ...), custom_call_target="tpu_custom_call", output_to_operand_aliasing={{}: (0, {})} | custom-call | flops 2097152 | bytes 14680064 | tf_op jit(solution)/shard_map/fold/pallas_call | solution.py:544
  (55 shorter events, 10.1 us)
Async XLA Ops:
  0.6 26.8 %copy-start.5 = (s32[16,2]{0,1:T(2,128)S(1)}, s32[16,2]{0,1:T(2,128)}, u32[]{:S(2)}) copy-start(s32[16,2]{0,1:T(2,128)} %param.9) | copy-start | bytes 388
  2.3 54.8 %collective-permute-start = (f32[2,128,1024]{2,1,0:T(8,128)S(1)}, f32[2,128,1024]{2,1,0:T(8,128)}, u32[]{:S(2)}, u32[]{:S(2)}) collective-permute-start(f32[2,128,1024]{2,1,0:T(8,128)S(1)} %get-tuple-element.40), channel_id=1, source_target_pairs={{0,4},{1,5},{2,6},{3,7},{4,8},{5,9},{6,10},{7,11},{8,12},{9,13},{1... | collective-permute-start | bytes 3145736 | tf_op jit(solution)/shard_map/ppermute | solution.py:572
  5.7 51.4 %collective-permute-start.1 = (f32[2,128,1024]{2,1,0:T(8,128)S(1)}, f32[2,128,1024]{2,1,0:T(8,128)}, u32[]{:S(2)}, u32[]{:S(2)}) collective-permute-start(f32[2,128,1024]{2,1,0:T(8,128)S(1)} %get-tuple-element.39), channel_id=1, source_target_pairs={{4,0},{5,1},{6,2},{7,3},{8,4},{9,5},{10,6},{11,7},{12,8},{13,9},{1... | collective-permute-start | bytes 3145736 | tf_op jit(solution)/shard_map/ppermute | solution.py:572
  8.2 16.0 %collective-permute-start.4 = (f32[2,128,128]{2,1,0:T(8,128)S(1)}, f32[2,128,128]{2,1,0:T(8,128)S(1)}, u32[]{:S(2)}, u32[]{:S(2)}) collective-permute-start(f32[2,128,128]{2,1,0:T(8,128)S(1)} %get-tuple-element.36), channel_id=1, source_target_pairs={{0,5},{1,6},{2,7},{4,9},{5,10},{6,11},{8,13},{9,14},{10,15},{12,17... | collective-permute-start | bytes 393224 | tf_op jit(solution)/shard_map/ppermute | solution.py:572
  13.5 12.0 %collective-permute-start.5 = (f32[2,128,128]{2,1,0:T(8,128)S(1)}, f32[2,128,128]{2,1,0:T(8,128)S(1)}, u32[]{:S(2)}, u32[]{:S(2)}) collective-permute-start(f32[2,128,128]{2,1,0:T(8,128)S(1)} %get-tuple-element.35), channel_id=1, source_target_pairs={{1,4},{2,5},{3,6},{5,8},{6,9},{7,10},{9,12},{10,13},{11,14},{13,16... | collective-permute-start | bytes 393224 | tf_op jit(solution)/shard_map/ppermute | solution.py:572
  16.9 40.3 %collective-permute-start.2 = (f32[2,1024,128]{2,1,0:T(8,128)}, f32[2,1024,128]{2,1,0:T(8,128)}, u32[]{:S(2)}, u32[]{:S(2)}) collective-permute-start(f32[2,1024,128]{2,1,0:T(8,128)} %get-tuple-element.38), channel_id=1, source_target_pairs={{0,1},{1,2},{2,3},{4,5},{5,6},{6,7},{8,9},{9,10},{10,11},{12,13},{... | collective-permute-start | bytes 3145736 | tf_op jit(solution)/shard_map/ppermute | solution.py:572
  24.2 25.5 %copy-start.6 = (f32[2,128,128]{2,1,0:T(8,128)}, f32[2,128,128]{2,1,0:T(8,128)S(1)}, u32[]{:S(2)}) copy-start(f32[2,128,128]{2,1,0:T(8,128)S(1)} %collective-permute-done.4.refs_9_) | copy-start | bytes 393220
  24.2 33.0 %collective-permute-start.3 = (f32[2,1024,128]{2,1,0:T(8,128)S(1)}, f32[2,1024,128]{2,1,0:T(8,128)}, u32[]{:S(2)}, u32[]{:S(2)}) collective-permute-start(f32[2,1024,128]{2,1,0:T(8,128)S(1)} %get-tuple-element.37), channel_id=1, source_target_pairs={{1,0},{2,1},{3,2},{5,4},{6,5},{7,6},{9,8},{10,9},{11,10},{13,12},{... | collective-permute-start | bytes 3145736 | tf_op jit(solution)/shard_map/ppermute | solution.py:572
  25.5 0.7 copy-start.7
  26.2 2.0 %collective-permute-start.6 = (f32[2,128,128]{2,1,0:T(8,128)S(1)}, f32[2,128,128]{2,1,0:T(8,128)}, u32[]{:S(2)}, u32[]{:S(2)}) collective-permute-start(f32[2,128,128]{2,1,0:T(8,128)S(1)} %get-tuple-element.34), channel_id=1, source_target_pairs={{4,1},{5,2},{6,3},{8,5},{9,6},{10,7},{12,9},{13,10},{14,11},{16,13... | collective-permute-start | bytes 393224 | tf_op jit(solution)/shard_map/ppermute | solution.py:572
  28.2 29.0 %collective-permute-start.7 = (f32[2,128,128]{2,1,0:T(8,128)S(1)}, f32[2,128,128]{2,1,0:T(8,128)S(1)}, u32[]{:S(2)}, u32[]{:S(2)}) collective-permute-start(f32[2,128,128]{2,1,0:T(8,128)S(1)} %get-tuple-element.33), channel_id=1, source_target_pairs={{5,0},{6,1},{7,2},{9,4},{10,5},{11,6},{13,8},{14,9},{15,10},{17,12... | collective-permute-start | bytes 393224 | tf_op jit(solution)/shard_map/ppermute | solution.py:572
  57.1 0.7 copy-start.8
  76.4 25.3 %collective-permute-start.16 = (f32[512,128]{1,0:T(8,128)S(1)}, f32[512,128]{1,0:T(8,128)S(1)}, u32[]{:S(2)}, u32[]{:S(2)}) collective-permute-start(f32[512,128]{1,0:T(8,128)S(1)} %constant_dynamic-slice_fusion.6), channel_id=1, source_target_pairs={{0,4},{4,0},{8,12},{12,8},{16,20},{20,16},{24,28},{28,24},{1,5},{5... | collective-permute-start | bytes 786440 | tf_op jit(solution)/shard_map/ppermute | solution.py:430
  102.7 4.6 %collective-permute-start.19 = (f32[128,128]{1,0:T(8,128)S(1)}, f32[128,128]{1,0:T(8,128)S(1)}, u32[]{:S(2)}, u32[]{:S(2)}) collective-permute-start(f32[128,128]{1,0:T(8,128)S(1)} %get-tuple-element.42), channel_id=1, source_target_pairs={{0,24},{4,28},{8,0},{12,4},{16,8},{20,12},{24,16},{28,20},{1,25},{... | collective-permute-start | bytes 196616 | tf_op jit(solution)/shard_map/ppermute | solution.py:430
  102.8 5.8 %collective-permute-start.18 = (f32[128,128]{1,0:T(8,128)S(1)}, f32[128,128]{1,0:T(8,128)S(1)}, u32[]{:S(2)}, u32[]{:S(2)}) collective-permute-start(f32[128,128]{1,0:T(8,128)S(1)} %get-tuple-element.43), channel_id=1, source_target_pairs={{0,16},{4,20},{8,24},{12,28},{16,0},{20,4},{24,8},{28,12},{1,17},{... | collective-permute-start | bytes 196616 | tf_op jit(solution)/shard_map/ppermute | solution.py:430
  102.9 5.8 %collective-permute-start.17 = (f32[128,128]{1,0:T(8,128)S(1)}, f32[128,128]{1,0:T(8,128)S(1)}, u32[]{:S(2)}, u32[]{:S(2)}) collective-permute-start(f32[128,128]{1,0:T(8,128)S(1)} %get-tuple-element.41), channel_id=1, source_target_pairs={{0,8},{4,12},{8,16},{12,20},{16,24},{20,28},{24,0},{28,4},{1,9},{5... | collective-permute-start | bytes 196616 | tf_op jit(solution)/shard_map/ppermute | solution.py:430
  108.7 8.7 %collective-permute-start.22 = (f32[32,128]{1,0:T(8,128)S(1)}, f32[32,128]{1,0:T(8,128)S(1)}, u32[]{:S(2)}, u32[]{:S(2)}) collective-permute-start(f32[32,128]{1,0:T(8,128)S(1)} %get-tuple-element.45), channel_id=1, source_target_pairs={{0,3},{1,0},{2,1},{3,2},{4,7},{5,4},{6,5},{7,6},{8,11},{9,8},{10,9... | collective-permute-start | bytes 49160 | tf_op jit(solution)/shard_map/ppermute | solution.py:430
  111.3 6.1 %collective-permute-start.21 = (f32[32,128]{1,0:T(8,128)S(1)}, f32[32,128]{1,0:T(8,128)S(1)}, u32[]{:S(2)}, u32[]{:S(2)}) collective-permute-start(f32[32,128]{1,0:T(8,128)S(1)} %get-tuple-element.46), channel_id=1, source_target_pairs={{0,2},{1,3},{2,0},{3,1},{4,6},{5,7},{6,4},{7,5},{8,10},{9,11},{10,... | collective-permute-start | bytes 49160 | tf_op jit(solution)/shard_map/ppermute | solution.py:430
  115.5 5.5 %collective-permute-start.20 = (f32[32,128]{1,0:T(8,128)S(1)}, f32[32,128]{1,0:T(8,128)S(1)}, u32[]{:S(2)}, u32[]{:S(2)}) collective-permute-start(f32[32,128]{1,0:T(8,128)S(1)} %get-tuple-element.44), channel_id=1, source_target_pairs={{0,1},{1,2},{2,3},{3,0},{4,5},{5,6},{6,7},{7,4},{8,9},{9,10},{10,1... | collective-permute-start | bytes 49160 | tf_op jit(solution)/shard_map/ppermute | solution.py:430
  122.3 6.3 %collective-permute-start.23 = (f32[32,128]{1,0:T(8,128)S(1)}, f32[32,128]{1,0:T(8,128)S(1)}, u32[]{:S(2)}, u32[]{:S(2)}) collective-permute-start(f32[32,128]{1,0:T(8,128)S(1)} %get-tuple-element.32), channel_id=1, source_target_pairs={{0,1},{1,2},{2,3},{3,0},{4,5},{5,6},{6,7},{7,4},{8,9},{9,10},{10,1... | collective-permute-start | bytes 49160 | tf_op jit(solution)/shard_map/ppermute | solution.py:430
  122.4 56.9 %collective-permute-start.8 = (f32[2,128,1024]{2,1,0:T(8,128)}, f32[2,128,1024]{2,1,0:T(8,128)S(1)}, u32[]{:S(2)}, u32[]{:S(2)}) collective-permute-start(f32[2,128,1024]{2,1,0:T(8,128)} %get-tuple-element.21), channel_id=1, source_target_pairs={{0,4},{1,5},{2,6},{3,7},{4,8},{5,9},{6,10},{7,11},{8,12},{9,13},{1... | collective-permute-start | bytes 3145736 | tf_op jit(solution)/shard_map/ppermute | solution.py:572
  123.8 55.6 %collective-permute-start.9 = (f32[2,128,1024]{2,1,0:T(8,128)}, f32[2,128,1024]{2,1,0:T(8,128)S(1)}, u32[]{:S(2)}, u32[]{:S(2)}) collective-permute-start(f32[2,128,1024]{2,1,0:T(8,128)} %get-tuple-element.22), channel_id=1, source_target_pairs={{4,0},{5,1},{6,2},{7,3},{8,4},{9,5},{10,6},{11,7},{12,8},{13,9},{1... | collective-permute-start | bytes 3145736 | tf_op jit(solution)/shard_map/ppermute | solution.py:572
  125.1 16.7 %collective-permute-start.12 = (f32[2,128,128]{2,1,0:T(8,128)}, f32[2,128,128]{2,1,0:T(8,128)S(1)}, u32[]{:S(2)}, u32[]{:S(2)}) collective-permute-start(f32[2,128,128]{2,1,0:T(8,128)} %get-tuple-element.25), channel_id=1, source_target_pairs={{0,5},{1,6},{2,7},{4,9},{5,10},{6,11},{8,13},{9,14},{10,15},{12,17... | collective-permute-start | bytes 393224 | tf_op jit(solution)/shard_map/ppermute | solution.py:572
  127.9 17.8 %collective-permute-start.13 = (f32[2,128,128]{2,1,0:T(8,128)}, f32[2,128,128]{2,1,0:T(8,128)S(1)}, u32[]{:S(2)}, u32[]{:S(2)}) collective-permute-start(f32[2,128,128]{2,1,0:T(8,128)} %get-tuple-element.26), channel_id=1, source_target_pairs={{1,4},{2,5},{3,6},{5,8},{6,9},{7,10},{9,12},{10,13},{11,14},{13,16... | collective-permute-start | bytes 393224 | tf_op jit(solution)/shard_map/ppermute | solution.py:572
  128.6 9.0 %collective-permute-start.24 = (f32[32,128]{1,0:T(8,128)S(1)}, f32[32,128]{1,0:T(8,128)S(1)}, u32[]{:S(2)}, u32[]{:S(2)}) collective-permute-start(f32[32,128]{1,0:T(8,128)S(1)} %get-tuple-element.32), channel_id=1, source_target_pairs={{0,2},{1,3},{2,0},{3,1},{4,6},{5,7},{6,4},{7,5},{8,10},{9,11},{10,... | collective-permute-start | bytes 49160 | tf_op jit(solution)/shard_map/ppermute | solution.py:430
  137.6 6.2 %collective-permute-start.25 = (f32[32,128]{1,0:T(8,128)S(1)}, f32[32,128]{1,0:T(8,128)S(1)}, u32[]{:S(2)}, u32[]{:S(2)}) collective-permute-start(f32[32,128]{1,0:T(8,128)S(1)} %get-tuple-element.32), channel_id=1, source_target_pairs={{0,3},{1,0},{2,1},{3,2},{4,7},{5,4},{6,5},{7,6},{8,11},{9,8},{10,9... | collective-permute-start | bytes 49160 | tf_op jit(solution)/shard_map/ppermute | solution.py:430
  141.8 37.6 %collective-permute-start.10 = (f32[2,1024,128]{2,1,0:T(8,128)}, f32[2,1024,128]{2,1,0:T(8,128)S(1)}, u32[]{:S(2)}, u32[]{:S(2)}) collective-permute-start(f32[2,1024,128]{2,1,0:T(8,128)} %get-tuple-element.23), channel_id=1, source_target_pairs={{0,1},{1,2},{2,3},{4,5},{5,6},{6,7},{8,9},{9,10},{10,11},{12,13},{... | collective-permute-start | bytes 3145736 | tf_op jit(solution)/shard_map/ppermute | solution.py:572
  143.8 35.6 %collective-permute-start.11 = (f32[2,1024,128]{2,1,0:T(8,128)}, f32[2,1024,128]{2,1,0:T(8,128)}, u32[]{:S(2)}, u32[]{:S(2)}) collective-permute-start(f32[2,1024,128]{2,1,0:T(8,128)} %get-tuple-element.24), channel_id=1, source_target_pairs={{1,0},{2,1},{3,2},{5,4},{6,5},{7,6},{9,8},{10,9},{11,10},{13,12},{... | collective-permute-start | bytes 3145736 | tf_op jit(solution)/shard_map/ppermute | solution.py:572
  145.7 0.7 copy-start
  146.4 5.5 %collective-permute-start.26 = (f32[128,128]{1,0:T(8,128)}, f32[128,128]{1,0:T(8,128)S(1)}, u32[]{:S(2)}, u32[]{:S(2)}) collective-permute-start(f32[128,128]{1,0:T(8,128)} %constant_dynamic-update-slice_fusion.4), channel_id=1, source_target_pairs={{0,8},{4,12},{8,16},{12,20},{16,24},{20,28},{24,0},{28,4},{1,9},{5... | collective-permute-start | bytes 196616 | tf_op jit(solution)/shard_map/ppermute | solution.py:430
  151.9 0.6 copy-start.4
  152.5 5.5 %collective-permute-start.27 = (f32[128,128]{1,0:T(8,128)}, f32[128,128]{1,0:T(8,128)S(1)}, u32[]{:S(2)}, u32[]{:S(2)}) collective-permute-start(f32[128,128]{1,0:T(8,128)} %constant_dynamic-update-slice_fusion.4), channel_id=1, source_target_pairs={{0,16},{4,20},{8,24},{12,28},{16,0},{20,4},{24,8},{28,12},{1,17},{... | collective-permute-start | bytes 196616 | tf_op jit(solution)/shard_map/ppermute | solution.py:430
  158.0 4.5 %collective-permute-start.28 = (f32[128,128]{1,0:T(8,128)}, f32[128,128]{1,0:T(8,128)S(1)}, u32[]{:S(2)}, u32[]{:S(2)}) collective-permute-start(f32[128,128]{1,0:T(8,128)} %constant_dynamic-update-slice_fusion.4), channel_id=1, source_target_pairs={{0,24},{4,28},{8,0},{12,4},{16,8},{20,12},{24,16},{28,20},{1,25},{... | collective-permute-start | bytes 196616 | tf_op jit(solution)/shard_map/ppermute | solution.py:430
  162.5 0.7 collective-permute-start.14
  163.2 0.7 copy-start.2
  163.8 6.8 %collective-permute-start.29 = (f32[512,128]{1,0:T(8,128)S(1)}, f32[512,128]{1,0:T(8,128)}, u32[]{:S(2)}, u32[]{:S(2)}) collective-permute-start(f32[512,128]{1,0:T(8,128)S(1)} %constant_dynamic-update-slice_fusion.refs_0_), channel_id=1, source_target_pairs={{0,4},{4,0},{8,12},{12,8},{16,20},{20,16},{24,28},{28,24},{1,5},{5... | collective-permute-start | bytes 786440 | tf_op jit(solution)/shard_map/ppermute | solution.py:430
  170.6 8.7 %collective-permute-start.15 = (f32[2,128,128]{2,1,0:T(8,128)}, f32[2,128,128]{2,1,0:T(8,128)S(1)}, u32[]{:S(2)}, u32[]{:S(2)}) collective-permute-start(f32[2,128,128]{2,1,0:T(8,128)} %get-tuple-element.28), channel_id=1, source_target_pairs={{5,0},{6,1},{7,2},{9,4},{10,5},{11,6},{13,8},{14,9},{15,10},{17,12... | collective-permute-start | bytes 393224 | tf_op jit(solution)/shard_map/ppermute | solution.py:572
  179.4 0.9 copy-start.1
  180.3 0.9 copy-start.3
where the time goes:
time: 189 us; the launch traced here: 186 us
  starting transfers between devices  89.6 us (47%)
  Pallas kernels  44.2 us (23%)
  waiting for transfers between devices  31.3 us (17%)
  local copies, waits for them, and re-layouts  16.4 us (9%)
  other arithmetic  3.16 us (2%)
    ppermute x14, starting transfers between devices, send(): return lax.ppermute(y, axis, pairs)  56.4 us
    pallas_call x2, Pallas kernels, run_slots(): pl.pallas_call(functools.partial(slot_kernel, phase, extent, slots, tile)...  37.9 us
    ppermute x16, starting transfers between devices, shift2(): return lax.ppermute(x, ('gx', 'gy'), pairs)  33.2 us
    ppermute x14, waiting for transfers between devices, send(): return lax.ppermute(y, axis, pairs)  18.7 us
    ppermute x16, waiting for transfers between devices, shift2(): return lax.ppermute(x, ('gx', 'gy'), pairs)  12.6 us
    unnamed x19, local copies, waits for them, and re-layouts  5.68 us
    slice x3, local copies, waits for them, and re-layouts, bring(): return shift2(object_field[:, end(dx), end(dy)], dx, dy)  5.54 us
    pallas_call x1, Pallas kernels, fold(): pl.pallas_call(functools.partial(fold_kernel, half, tile), out_shape=jax....  4.48 us
  transfers between devices with their start and end apart: 30, of which 11 were waited for; matrix products, arithmetic and copies ran while one was open for 5% of the time, Pallas kernels for 12%

commit v1 on v0

--- a/solution.py
+++ b/solution.py
@@ -61,17 +61,19 @@
     take = lambda n: [next(it) for _ in range(n)]
     tile_hbm, probe, meas_hbm, mats, pick = take(5)
     if not inner:
-        sides_hbm, corners_hbm = take(4), take(4)
+        sides_hbm = take(4)
         grad_in, acc_in, loss_in = take(3)
         del grad_in
     grad_out, acc_out, loss_out = take(3)
     if not inner:
-        gsides, gcorners = take(4), take(4)
+        gsides = take(8)
     ext, grad, shifted, accs, turned, kept, meas, sh_h, sh_l, z_h, z_l, sems, msems, order = take(14)
     mid = pl.ds(half, tile)
     low, high = pl.ds(0, half), pl.ds(half + tile, half)
-    sides = ((low, mid), (high, mid), (mid, low), (mid, high))
-    corners = ((low, low), (low, high), (high, low), (high, high))
+    whole = pl.ds(0, 2 * half + tile)
+    sides_in = ((low, whole), (high, whole), (mid, low), (mid, high))
+    sides_out = ((low, mid), (high, mid), (mid, low), (mid, high))
+    sides_out += ((low, low), (low, high), (high, low), (high, high))
     band = min(extent, tile // 2)
     rest = tile - 2 * band
     ring = [(0, band, 0, tile), (tile - band, band, 0, tile)]
@@ -99,7 +101,7 @@
     if inner:
         copy(tile_hbm, ext.at[:, mid, mid])
     else:
-        for src, (rows, cols) in zip(sides_hbm + corners_hbm, sides + corners):
+        for src, (rows, cols) in zip(sides_hbm, sides_in):
             copy(src, ext.at[:, rows, cols])
         for box in ring:
             copy(own(tile_hbm, box, 0), own(ext, box, half))
@@ -144,7 +146,7 @@
         clear(mid, mid)
     else:
         loss_out[...] = loss_in[...]
-        for rows, cols in sides + corners:
+        for rows, cols in sides_in:
             clear(rows, cols)
     for c in loads:
         c.wait()
@@ -353,7 +355,7 @@
     if inner:
         copy(grad.at[:, mid, mid], grad_out)
     else:
-        for dst, (rows, cols) in zip(gsides + gcorners, sides + corners):
+        for dst, (rows, cols) in zip(gsides, sides_out):
             copy(grad.at[:, rows, cols], dst)
         for box in ring:
             copy(own(grad, box, half), own(grad_out, box, 0))
@@ -387,7 +389,7 @@
     ]
     out_specs = [hbm, vmem, vmem]
     if not inner:
-        in_specs += [hbm] * 9 + [vmem, vmem]
+        in_specs += [hbm] * 5 + [vmem, vmem]
         out_shape += [jax.ShapeDtypeStruct((2, half, tile), F32)] * 2
         out_shape += [jax.ShapeDtypeStruct((2, tile, half), F32)] * 2
         out_shape += [jax.ShapeDtypeStruct((2, half, half), F32)] * 4
@@ -420,20 +422,21 @@
     )(centers, live, tile_obj, probe, measured, *tables, *extra)
 
 
+def send(y, axis, stride, count, k):
+    n = lax.axis_size(axis)
+    spot = lambda i: (i // stride) % count
+    pairs = [(i, i + ((spot(i) + k) % count - spot(i)) * stride) for i in range(n)]
+    return lax.ppermute(y, axis, pairs)
+
+
 def sum_all(x, groups, scale, shape):
     flat = x
-
-    def send(y, axis, stride, count, k):
-        n = lax.axis_size(axis)
-        spot = lambda i: (i // stride) % count
-        pairs = [(i, i + ((spot(i) + k) % count - spot(i)) * stride) for i in range(n)]
-        return lax.ppermute(y, axis, pairs)
-
-    def place(axis, stride, count):
-        return lax.rem(lax.axis_index(axis) // stride, count)
-
-    for axis, stride, count in groups:
-        me = place(axis, stride, count)
+    axis, stride, last = groups[-1]
+    whole = last & (last - 1) == 0
+    split = groups[:-1] if whole else groups
+    places = [lax.rem(lax.axis_index(axis) // stride, count) for axis, stride, count in split]
+    for level, (axis, stride, count) in enumerate(split):
+        me = places[level]
         rows = flat.shape[0] // count
         own = lax.dynamic_slice_in_dim(flat, me * rows, rows, 0)
         got = [
@@ -441,9 +444,16 @@
             for k in range(1, count)
         ]
         flat = sum(got, own)
-    for level, (axis, stride, count) in reversed(list(enumerate(groups))):
+    if whole:
+        axis, stride, count = groups[-1]
+        n = lax.axis_size(axis)
+        tree = [flat] + [lax.ppermute(flat, axis, [(i, i ^ (k * stride)) for i in range(n)]) for k in range(1, count)]
+        while len(tree) > 1:
+            tree = [tree[k] + tree[k + 1] for k in range(0, len(tree), 2)]
+        flat = tree[0]
+    for level, (axis, stride, count) in reversed(list(enumerate(split))):
+        me = places[level]
         pieces = [flat] + [send(flat, axis, stride, count, k) for k in range(1, count)]
-        me = place(axis, stride, count)
         if level == 0 and count == 2:
             return finish(me, pieces, scale, shape)
         rows = flat.shape[0]
@@ -486,7 +496,8 @@
 
 
 def fold_kernel(half, tile, main, *refs):
-    adds, corners = refs[:4], refs[4:8]
+    adds = refs[:4]
+    corners = refs[4:8]
     out, rows_buf, cols_buf, rows_add, cols_add, corner_add, sems = refs[8:]
     del main
     inside = tile - 2 * half
@@ -572,10 +583,6 @@
     return lax.ppermute(x, ("gx", "gy"), pairs)
 
 
-SIDES = ((1, 0), (-1, 0), (0, 1), (0, -1))
-CORNERS = ((1, 1), (1, -1), (-1, 1), (-1, -1))
-
-
 def on_device(object_field, probe, centers, live, measured):
     extent = probe.shape[1]
     half = extent // 2
@@ -583,35 +590,29 @@
     slots = centers.shape[0]
     tables = [jnp.asarray(t) for t in tables_np(extent)]
     far = tile - half
-
-    def end(step):
-        if step == 0:
-            return slice(None)
-        return slice(far, tile) if step == 1 else slice(0, half)
-
-    def bring(dx, dy):
-        return shift2(object_field[:, end(dx), end(dy)], dx, dy)
-
-    left, right = bring(0, 1), bring(0, -1)
-    up, down = bring(1, 0), bring(-1, 0)
-
-    corners = [bring(dx, dy) for dx, dy in CORNERS]
+    ends = (slice(0, half), slice(far, tile))
+
+    end_left = shift2(jnp.stack([object_field[:, e, far:] for e in ends]), 0, 1)
+    end_right = shift2(jnp.stack([object_field[:, e, :half] for e in ends]), 0, -1)
+    left = shift2(object_field[:, :, far:], 0, 1)
+    right = shift2(object_field[:, :, :half], 0, -1)
+    edges = [jnp.concatenate([end_left[k], object_field[:, ends[k]], end_right[k]], axis=2) for k in range(2)]
+    up = shift2(edges[1], 1, 0)
+    down = shift2(edges[0], -1, 0)
     grad_a, acc_a, loss_a = run_slots("inner", centers, live, object_field, probe, measured, tables)
-    out = run_slots(
+    grad_b, acc_b, loss_b, gup, gdown, gleft, gright, *gcorners = run_slots(
         "outer", centers, live, object_field, probe, measured, tables,
-        (up, down, left, right, *corners, grad_a, acc_a, loss_a),
+        (up, down, left, right, grad_a, acc_a, loss_a),
     )
-    grad_b, acc_b, loss_b = out[:3]
-    sent = {}
-    for places in ((2, 3), (0, 1), (4, 5, 6, 7)):
-        for k in places:
-            dx, dy = (SIDES + CORNERS)[k]
-            sent[k] = shift2(out[3 + k], -dx, -dy)
-    sides = [sent[1], sent[0], sent[3], sent[2]]
-    corners = [sent[7], sent[6], sent[5], sent[4]]
+    from_left = shift2(gright, 0, 1)
+    from_right = shift2(gleft, 0, -1)
+    from_up = shift2(gdown, 1, 0)
+    from_down = shift2(gup, -1, 0)
+    steps = ((-1, -1), (-1, 1), (1, -1), (1, 1))
+    corners = [shift2(g, dx, dy) for g, (dx, dy) in zip(gcorners, steps)][::-1]
     slots_all = slots * lax.axis_size("gx") * lax.axis_size("gy")
     probe_grad = sum_all(acc_b, sum_groups(), 1.0 / math.sqrt(slots_all), probe.shape)
-    object_grad = fold(grad_b, sides, corners)
+    object_grad = fold(grad_b, (from_up, from_down, from_left, from_right), corners)
 
     slot_loss = jnp.sum(loss_b, axis=(1, 2)) * (0.5 / (extent * extent))
     return object_grad, probe_grad, slot_loss

time: 189 us -> 175 us (0.926)
  waiting for transfers between devices: 31.3 us -> 22.5 us
  local copies, waits for them, and re-layouts: 16.4 us -> 11.4 us
    ppermute x14 -> x8, waiting for transfers between devices: 18.7 us -> 9.76 us  [send(): return lax.ppermute(y, axis, pairs)]
    ppermute x14 -> x8, starting transfers between devices: 56.4 us -> 49.4 us  [send(): return lax.ppermute(y, axis, pairs)]
    ppermute x0 -> x3, starting transfers between devices: none -> 6.06 us  [sum_all(): lax.ppermute(flat, axis, [(i, i ^ k * stride) for i in range(n)])]
    dynamic_update_slice x7 -> x3, local copies, waits for them, and re-layouts: 3.55 us -> 0.03 us  [sum_all(): lax.dynamic_update_slice_in_dim(out, piece, lax.rem(me + count - k, count...]
    slice x3 -> x2, local copies, waits for them, and re-layouts: 5.54 us -> 4.72 us  [the longest x1 3.04 us: on_device(): right = shift2(object_field[:, :, :half], 0, -1)]
    ppermute x16 -> x14, starting transfers between devices: 33.2 us -> 33.5 us  [shift2(): return lax.ppermute(x, ('gx', 'gy'), pairs)]
    ppermute x16 -> x14, waiting for transfers between devices: 12.6 us -> 12.7 us  [shift2(): return lax.ppermute(x, ('gx', 'gy'), pairs)]
  transfers between devices with their start and end apart: 30 -> 25, of which waited for: 11 -> 9; matrix products, arithmetic and copies ran while one was open for 5% -> 5% of each run, Pallas kernels for 12% -> 13%
where the time goes in v1:
time: 175 us; the launch traced here: 172 us
  starting transfers between devices  89 us (51%)
  Pallas kernels  44.1 us (25%)
  waiting for transfers between devices  22.5 us (13%)
  local copies, waits for them, and re-layouts  11.4 us (7%)
  other arithmetic  4.36 us (2%)
    ppermute x8, starting transfers between devices, send(): return lax.ppermute(y, axis, pairs)  49.4 us
    pallas_call x2, Pallas kernels, run_slots(): pl.pallas_call(functools.partial(slot_kernel, phase, extent, slots, tile)...  37.8 us
    ppermute x14, starting transfers between devices, shift2(): return lax.ppermute(x, ('gx', 'gy'), pairs)  33.5 us
    ppermute x14, waiting for transfers between devices, shift2(): return lax.ppermute(x, ('gx', 'gy'), pairs)  12.7 us
    ppermute x8, waiting for transfers between devices, send(): return lax.ppermute(y, axis, pairs)  9.76 us
    ppermute x3, starting transfers between devices, sum_all(): lax.ppermute(flat, axis, [(i, i ^ k * stride) for i in range(n)])  6.06 us
    pallas_call x1, Pallas kernels, fold(): pl.pallas_call(functools.partial(fold_kernel, half, tile), out_shape=jax....  4.48 us
    unnamed x19, local copies, waits for them, and re-layouts  4.38 us
  transfers between devices with their start and end apart: 25, of which 9 were waited for; matrix products, arithmetic and copies ran while one was open for 5% of the time, Pallas kernels for 13%

profile of v1, /device:TPU:0, one launch (start us, length us, event | category | flops | bytes accessed | tf_op | source)
XLA Modules:
  0.0 172.4 jit_solution(14329983334312794212)
XLA Ops:
  0.6 1.2 slice_bitcast_fusion.7
  1.8 1.3 collective-permute-start.1
  3.1 5.6 %collective-permute-start = (f32[2,2,128,128]{3,2,1,0:T(8,128)S(1)}, f32[2,2,128,128]{3,2,1,0:T(8,128)S(1)}, u32[]{:S(2)}, u32[]{:S(2)}) collective-permute-start(f32[2,2,128,128]{3,2,1,0:T(8,128)S(1)} %pad_maximum_fusion.2), channel_id=1, source_target_pairs={{0,1},{1,2},{2,3},{4,5},{5,6},{6,7},{8,9},{9,10},{10,11},{12,13},{... | collective-permute-start | bytes 786440 | tf_op jit(solution)/shard_map/ppermute | solution.py:583
  8.7 1.7 fusion.1
  10.4 2.6 %collective-permute-done.1 = f32[2,2,128,128]{3,2,1,0:T(8,128)S(1)} collective-permute-done((f32[2,2,128,128]{3,2,1,0:T(8,128)S(1)}, f32[2,2,128,128]{3,2,1,0:T(8,128)S(1)}, u32[]{:S(2)}, u32[]{:S(2)}) %collective-permute-start.1) | collective-permute-done | bytes 262176 | tf_op jit(solution)/shard_map/ppermute | solution.py:583
  13.1 1.2 collective-permute-done
  14.4 2.4 %collective-permute-start.2 = (f32[2,128,1280]{2,1,0:T(8,128)S(1)}, f32[2,128,1280]{2,1,0:T(8,128)}, u32[]{:S(2)}, u32[]{:S(2)}) collective-permute-start(f32[2,128,1280]{2,1,0:T(8,128)S(1)} %pad_maximum_fusion), channel_id=1, source_target_pairs={{0,4},{1,5},{2,6},{3,7},{4,8},{5,9},{6,10},{7,11},{8,12},{9,13},{1... | collective-permute-start | bytes 3932168 | tf_op jit(solution)/shard_map/ppermute | solution.py:583
  16.9 1.3 collective-permute-start.3
  18.2 3.0 %fusion = (f32[2,1024,128]{2,1,0:T(8,128)}, f32[2,1024,128]{2,1,0:T(8,128)}) fusion(f32[2,1024,1024]{2,1,0:T(8,128)} %refs_0_.3), kind=kLoop, calls=%fused_computation.24 | loop fusion | bytes 4194304 | tf_op jit(solution)/shard_map/slice | solution.py:598
  21.2 5.4 %collective-permute-start.4 = (f32[2,1024,128]{2,1,0:T(8,128)}, f32[2,1024,128]{2,1,0:T(8,128)}, u32[]{:S(2)}, u32[]{:S(2)}) collective-permute-start(f32[2,1024,128]{2,1,0:T(8,128)} %get-tuple-element.34), channel_id=1, source_target_pairs={{0,1},{1,2},{2,3},{4,5},{5,6},{6,7},{8,9},{9,10},{10,11},{12,13},{... | collective-permute-start | bytes 3145736 | tf_op jit(solution)/shard_map/ppermute | solution.py:583
  26.6 1.3 collective-permute-start.5
  27.9 0.7 copy.13.centers
  28.6 20.2 %shard_map.94 = (f32[2,1024,1024]{2,1,0:T(8,128)}, f32[1024,128]{1,0:T(8,128)}, f32[16,8,128]{2,1,0:T(8,128)}) custom-call(s32[16,2]{1,0:T(8,128)} %copy.13.centers, s32[16]{0:T(128)} %live.3, f32[2,1024,1024]{2,1,0:T(8,128)} %refs_0_.3, f32[2,256,256]{2,1,0:T(8,128)} %refs_1_.3, f32[16,256,256]{2,1,0:T(8,128)} %refs_2_.3, ...), custom_call_target="tpu_custom_call" | custom-call | flops 8589934592 | bytes 33554432 | tf_op jit(solution)/shard_map/pallas_call | solution.py:398
  48.9 5.3 %collective-permute-done.5.refs_8_ = f32[2,1024,128]{2,1,0:T(8,128)} collective-permute-done((f32[2,1024,128]{2,1,0:T(8,128)}, f32[2,1024,128]{2,1,0:T(8,128)}, u32[]{:S(2)}, u32[]{:S(2)}) %collective-permute-start.5) | collective-permute-done | bytes 1048608 | tf_op jit(solution)/shard_map/ppermute | solution.py:583
  54.2 17.6 %shard_map.95 = (f32[2,1024,1024]{2,1,0:T(8,128)}, f32[1024,128]{1,0:T(8,128)}, f32[16,8,128]{2,1,0:T(8,128)}, f32[2,128,1024]{2,1,0:T(8,128)}, f32[2,128,1024]{...) custom-call(s32[16,2]{1,0:T(8,128)} %copy.13.centers, ...), custom_call_target="tpu_custom_call", output_to_operand_aliasing={{0}: (11, {})} | custom-call | flops 8589934592 | bytes 33554432 | tf_op jit(solution)/shard_map/pallas_call | solution.py:398
  71.8 1.0 constant_dynamic-slice_fusion.3
  72.8 8.6 %collective-permute-start.14 = (f32[512,128]{1,0:T(8,128)S(1)}, f32[512,128]{1,0:T(8,128)S(1)}, u32[]{:S(2)}, u32[]{:S(2)}) collective-permute-start(f32[512,128]{1,0:T(8,128)S(1)} %constant_dynamic-slice_fusion.3), channel_id=1, source_target_pairs={{0,4},{4,0},{8,12},{12,8},{16,20},{20,16},{24,28},{28,24},{1,5},{5... | collective-permute-start | bytes 786440 | tf_op jit(solution)/shard_map/ppermute | solution.py:429
  81.4 1.2 collective-permute-done.14
  82.6 1.0 dynamic-slice_add_fusion
  83.7 1.9 %collective-permute-start.15 = (f32[128,128]{1,0:T(8,128)S(1)}, f32[128,128]{1,0:T(8,128)S(1)}, u32[]{:S(2)}, u32[]{:S(2)}) collective-permute-start(f32[128,128]{1,0:T(8,128)S(1)} %get-tuple-element.41), channel_id=1, source_target_pairs={{0,8},{4,12},{8,16},{12,20},{16,24},{20,28},{24,0},{28,4},{1,9},{5... | collective-permute-start | bytes 196616 | tf_op jit(solution)/shard_map/ppermute | solution.py:429
  85.7 5.5 %collective-permute-start.10 = (f32[2,128,128]{2,1,0:T(8,128)S(1)}, f32[2,128,128]{2,1,0:T(8,128)S(1)}, u32[]{:S(2)}, u32[]{:S(2)}) collective-permute-start(f32[2,128,128]{2,1,0:T(8,128)S(1)} %copy-done.8), channel_id=1, source_target_pairs={{0,5},{1,6},{2,7},{4,9},{5,10},{6,11},{8,13},{9,14},{10,15},{12,17... | collective-permute-start | bytes 393224 | tf_op jit(solution)/shard_map/ppermute | solution.py:583
  91.2 0.6 add_add_fusion.1
  91.8 4.5 %collective-permute-start.19 = (f32[128,128]{1,0:T(8,128)}, f32[128,128]{1,0:T(8,128)S(1)}, u32[]{:S(2)}, u32[]{:S(2)}) collective-permute-start(f32[128,128]{1,0:T(8,128)} %add_add_fusion.1), channel_id=1, source_target_pairs={{0,2},{1,3},{2,0},{3,1},{4,6},{5,7},{6,4},{7,5},{8,10},{9,11},{10,... | collective-permute-start | bytes 196616 | tf_op jit(solution)/shard_map/ppermute | solution.py:450
  96.3 1.6 collective-permute-start.20
  97.9 1.9 %collective-permute-start.6 = (f32[2,128,1024]{2,1,0:T(8,128)}, f32[2,128,1024]{2,1,0:T(8,128)S(1)}, u32[]{:S(2)}, u32[]{:S(2)}) collective-permute-start(f32[2,128,1024]{2,1,0:T(8,128)} %get-tuple-element.21), channel_id=1, source_target_pairs={{0,4},{1,5},{2,6},{3,7},{4,8},{5,9},{6,10},{7,11},{8,12},{9,13},{1... | collective-permute-start | bytes 3145736 | tf_op jit(solution)/shard_map/ppermute | solution.py:583
  99.8 1.3 collective-permute-start.7
  101.1 0.6 copy-done.4
  101.8 3.7 %collective-permute-start.8 = (f32[2,1024,128]{2,1,0:T(8,128)}, f32[2,1024,128]{2,1,0:T(8,128)S(1)}, u32[]{:S(2)}, u32[]{:S(2)}) collective-permute-start(f32[2,1024,128]{2,1,0:T(8,128)} %get-tuple-element.23), channel_id=1, source_target_pairs={{0,1},{1,2},{2,3},{4,5},{5,6},{6,7},{8,9},{9,10},{10,11},{12,13},{... | collective-permute-start | bytes 3145736 | tf_op jit(solution)/shard_map/ppermute | solution.py:583
  105.5 1.3 collective-permute-start.9
  106.8 0.6 copy-done.6
  107.4 0.7 collective-permute-start.11
  108.1 1.0 constant_dynamic-update-slice_fusion.3
  109.1 28.6 %collective-permute-start.21 = (f32[128,128]{1,0:T(8,128)S(1)}, f32[128,128]{1,0:T(8,128)S(1)}, u32[]{:S(2)}, u32[]{:S(2)}) collective-permute-start(f32[128,128]{1,0:T(8,128)S(1)} %get-tuple-element.32), channel_id=1, source_target_pairs={{0,8},{4,12},{8,16},{12,20},{16,24},{20,28},{24,0},{28,4},{1,9},{5... | collective-permute-start | bytes 196616 | tf_op jit(solution)/shard_map/ppermute | solution.py:429
  137.6 2.4 %collective-permute-done.21 = f32[128,128]{1,0:T(8,128)S(1)} collective-permute-done((f32[128,128]{1,0:T(8,128)S(1)}, f32[128,128]{1,0:T(8,128)S(1)}, u32[]{:S(2)}, u32[]{:S(2)}) %collective-permute-start.21) | collective-permute-done | bytes 65568 | tf_op jit(solution)/shard_map/ppermute | solution.py:429
  140.0 5.2 %collective-permute-start.22 = (f32[128,128]{1,0:T(8,128)S(1)}, f32[128,128]{1,0:T(8,128)S(1)}, u32[]{:S(2)}, u32[]{:S(2)}) collective-permute-start(f32[128,128]{1,0:T(8,128)S(1)} %get-tuple-element.32), channel_id=1, source_target_pairs={{0,16},{4,20},{8,24},{12,28},{16,0},{20,4},{24,8},{28,12},{1,17},{... | collective-permute-start | bytes 196616 | tf_op jit(solution)/shard_map/ppermute | solution.py:429
  145.2 2.2 %collective-permute-done.22 = f32[128,128]{1,0:T(8,128)S(1)} collective-permute-done((f32[128,128]{1,0:T(8,128)S(1)}, f32[128,128]{1,0:T(8,128)S(1)}, u32[]{:S(2)}, u32[]{:S(2)}) %collective-permute-start.22) | collective-permute-done | bytes 65568 | tf_op jit(solution)/shard_map/ppermute | solution.py:429
  147.5 0.5 collective-permute-start.23
  148.0 3.7 %collective-permute-done.23 = f32[128,128]{1,0:T(8,128)S(1)} collective-permute-done((f32[128,128]{1,0:T(8,128)S(1)}, f32[128,128]{1,0:T(8,128)S(1)}, u32[]{:S(2)}, u32[]{:S(2)}) %collective-permute-start.23) | collective-permute-done | bytes 65568 | tf_op jit(solution)/shard_map/ppermute | solution.py:429
  151.7 0.7 collective-permute-start.12
  152.5 0.7 copy-done.2
  153.1 4.5 %collective-permute-start.24 = (f32[512,128]{1,0:T(8,128)S(1)}, f32[512,128]{1,0:T(8,128)}, u32[]{:S(2)}, u32[]{:S(2)}) collective-permute-start(f32[512,128]{1,0:T(8,128)S(1)} %constant_dynamic-update-slice_fusion.refs_0_), channel_id=1, source_target_pairs={{0,4},{4,0},{8,12},{12,8},{16,20},{20,16},{24,28},{28,24},{1,5},{5... | collective-permute-start | bytes 786440 | tf_op jit(solution)/shard_map/ppermute | solution.py:429
  157.6 1.0 reduce_sum.9
  158.9 1.3 collective-permute-start.13
  160.7 1.8 %finish.1 = f32[2,256,256]{2,1,0:T(8,128)} custom-call(s32[1]{0:T(128)} %bitcast.8.me, f32[512,128]{1,0:T(8,128)S(1)} %constant_dynamic-update-slice_fusion.refs_0_, f32[512,128]{1,0:T(8,128)} %collective-permute-done.24.refs_1_), custom_call_target="tpu_custom_call" | custom-call | flops 131072 | bytes 1048576 | tf_op jit(solution)/shard_map/finish/pallas_call | solution.py:481
  162.5 3.6 %collective-permute-done.13.refs_7_ = f32[2,128,128]{2,1,0:T(8,128)S(1)} collective-permute-done((f32[2,128,128]{2,1,0:T(8,128)}, f32[2,128,128]{2,1,0:T(8,128)S(1)}, u32[]{:S(2)}, u32[]{:S(2)}) %collective-permute-start.13) | collective-permute-done | bytes 131104 | tf_op jit(solution)/shard_map/ppermute | solution.py:583
  166.1 0.9 copy-done.1
  167.0 0.9 copy-done.3
  167.9 4.5 %fold.1 = f32[2,1024,1024]{2,1,0:T(8,128)} custom-call(f32[2,1024,1024]{2,1,0:T(8,128)} %get-tuple-element.20.main, f32[2,128,1024]{2,1,0:T(8,128)S(1)} %collective-permute-done.6.refs_0_, f32[2,128,1024]{2,1,0:T(8,128)S(1)} %collective-permute-done.7.refs_1_, f32[2,1024,128]{2,1,0:T(8,128)S(1)} %collective-permute-done.8.refs_2_, ...), custom_call_target="tpu_custom_call", output_to_operand_aliasing={{}: (0, {})} | custom-call | flops 2097152 | bytes 14680064 | tf_op jit(solution)/shard_map/fold/pallas_call | solution.py:555
  (45 shorter events, 1.3 us)
Async XLA Ops:
  1.8 11.3 %collective-permute-start.1 = (f32[2,2,128,128]{3,2,1,0:T(8,128)S(1)}, f32[2,2,128,128]{3,2,1,0:T(8,128)S(1)}, u32[]{:S(2)}, u32[]{:S(2)}) collective-permute-start(f32[2,2,128,128]{3,2,1,0:T(8,128)S(1)} %pad_maximum_fusion.3), channel_id=1, source_target_pairs={{1,0},{2,1},{3,2},{5,4},{6,5},{7,6},{9,8},{10,9},{11,10},{13,12},{... | collective-permute-start | bytes 786440 | tf_op jit(solution)/shard_map/ppermute | solution.py:583
  3.1 11.1 %collective-permute-start = (f32[2,2,128,128]{3,2,1,0:T(8,128)S(1)}, f32[2,2,128,128]{3,2,1,0:T(8,128)S(1)}, u32[]{:S(2)}, u32[]{:S(2)}) collective-permute-start(f32[2,2,128,128]{3,2,1,0:T(8,128)S(1)} %pad_maximum_fusion.2), channel_id=1, source_target_pairs={{0,1},{1,2},{2,3},{4,5},{5,6},{6,7},{8,9},{9,10},{10,11},{12,13},{... | collective-permute-start | bytes 786440 | tf_op jit(solution)/shard_map/ppermute | solution.py:583
  14.4 39.8 %collective-permute-start.2 = (f32[2,128,1280]{2,1,0:T(8,128)S(1)}, f32[2,128,1280]{2,1,0:T(8,128)}, u32[]{:S(2)}, u32[]{:S(2)}) collective-permute-start(f32[2,128,1280]{2,1,0:T(8,128)S(1)} %pad_maximum_fusion), channel_id=1, source_target_pairs={{0,4},{1,5},{2,6},{3,7},{4,8},{5,9},{6,10},{7,11},{8,12},{9,13},{1... | collective-permute-start | bytes 3932168 | tf_op jit(solution)/shard_map/ppermute | solution.py:583
  16.9 11.0 %copy-start.7 = (s32[16,2]{0,1:T(2,128)S(1)}, s32[16,2]{0,1:T(2,128)}, u32[]{:S(2)}) copy-start(s32[16,2]{0,1:T(2,128)} %param.9) | copy-start | bytes 388
  16.9 37.3 %collective-permute-start.3 = (f32[2,128,1280]{2,1,0:T(8,128)S(1)}, f32[2,128,1280]{2,1,0:T(8,128)}, u32[]{:S(2)}, u32[]{:S(2)}) collective-permute-start(f32[2,128,1280]{2,1,0:T(8,128)S(1)} %pad_maximum_fusion.1), channel_id=1, source_target_pairs={{4,0},{5,1},{6,2},{7,3},{8,4},{9,5},{10,6},{11,7},{12,8},{13,9},{1... | collective-permute-start | bytes 3932168 | tf_op jit(solution)/shard_map/ppermute | solution.py:583
  21.2 27.6 %collective-permute-start.4 = (f32[2,1024,128]{2,1,0:T(8,128)}, f32[2,1024,128]{2,1,0:T(8,128)}, u32[]{:S(2)}, u32[]{:S(2)}) collective-permute-start(f32[2,1024,128]{2,1,0:T(8,128)} %get-tuple-element.34), channel_id=1, source_target_pairs={{0,1},{1,2},{2,3},{4,5},{5,6},{6,7},{8,9},{9,10},{10,11},{12,13},{... | collective-permute-start | bytes 3145736 | tf_op jit(solution)/shard_map/ppermute | solution.py:583
  26.6 27.5 %collective-permute-start.5 = (f32[2,1024,128]{2,1,0:T(8,128)}, f32[2,1024,128]{2,1,0:T(8,128)}, u32[]{:S(2)}, u32[]{:S(2)}) collective-permute-start(f32[2,1024,128]{2,1,0:T(8,128)} %get-tuple-element.33), channel_id=1, source_target_pairs={{1,0},{2,1},{3,2},{5,4},{6,5},{7,6},{9,8},{10,9},{11,10},{13,12},{... | collective-permute-start | bytes 3145736 | tf_op jit(solution)/shard_map/ppermute | solution.py:583
  71.8 13.9 %copy-start.8 = (f32[2,128,128]{2,1,0:T(8,128)S(1)}, f32[2,128,128]{2,1,0:T(8,128)}, u32[]{:S(2)}) copy-start(f32[2,128,128]{2,1,0:T(8,128)} %get-tuple-element.25) | copy-start | bytes 393220
  72.8 9.8 %collective-permute-start.14 = (f32[512,128]{1,0:T(8,128)S(1)}, f32[512,128]{1,0:T(8,128)S(1)}, u32[]{:S(2)}, u32[]{:S(2)}) collective-permute-start(f32[512,128]{1,0:T(8,128)S(1)} %constant_dynamic-slice_fusion.3), channel_id=1, source_target_pairs={{0,4},{4,0},{8,12},{12,8},{16,20},{20,16},{24,28},{28,24},{1,5},{5... | collective-permute-start | bytes 786440 | tf_op jit(solution)/shard_map/ppermute | solution.py:429
  83.6 7.6 %collective-permute-start.17 = (f32[128,128]{1,0:T(8,128)S(1)}, f32[128,128]{1,0:T(8,128)S(1)}, u32[]{:S(2)}, u32[]{:S(2)}) collective-permute-start(f32[128,128]{1,0:T(8,128)S(1)} %get-tuple-element.42), channel_id=1, source_target_pairs={{0,24},{4,28},{8,0},{12,4},{16,8},{20,12},{24,16},{28,20},{1,25},{... | collective-permute-start | bytes 196616 | tf_op jit(solution)/shard_map/ppermute | solution.py:429
  83.6 7.5 %collective-permute-start.16 = (f32[128,128]{1,0:T(8,128)S(1)}, f32[128,128]{1,0:T(8,128)S(1)}, u32[]{:S(2)}, u32[]{:S(2)}) collective-permute-start(f32[128,128]{1,0:T(8,128)S(1)} %get-tuple-element.43), channel_id=1, source_target_pairs={{0,16},{4,20},{8,24},{12,28},{16,0},{20,4},{24,8},{28,12},{1,17},{... | collective-permute-start | bytes 196616 | tf_op jit(solution)/shard_map/ppermute | solution.py:429
  83.7 7.5 %collective-permute-start.15 = (f32[128,128]{1,0:T(8,128)S(1)}, f32[128,128]{1,0:T(8,128)S(1)}, u32[]{:S(2)}, u32[]{:S(2)}) collective-permute-start(f32[128,128]{1,0:T(8,128)S(1)} %get-tuple-element.41), channel_id=1, source_target_pairs={{0,8},{4,12},{8,16},{12,20},{16,24},{20,28},{24,0},{28,4},{1,9},{5... | collective-permute-start | bytes 196616 | tf_op jit(solution)/shard_map/ppermute | solution.py:429
  85.7 14.1 %collective-permute-start.10 = (f32[2,128,128]{2,1,0:T(8,128)S(1)}, f32[2,128,128]{2,1,0:T(8,128)S(1)}, u32[]{:S(2)}, u32[]{:S(2)}) collective-permute-start(f32[2,128,128]{2,1,0:T(8,128)S(1)} %copy-done.8), channel_id=1, source_target_pairs={{0,5},{1,6},{2,7},{4,9},{5,10},{6,11},{8,13},{9,14},{10,15},{12,17... | collective-permute-start | bytes 393224 | tf_op jit(solution)/shard_map/ppermute | solution.py:583
  91.8 9.3 %collective-permute-start.19 = (f32[128,128]{1,0:T(8,128)}, f32[128,128]{1,0:T(8,128)S(1)}, u32[]{:S(2)}, u32[]{:S(2)}) collective-permute-start(f32[128,128]{1,0:T(8,128)} %add_add_fusion.1), channel_id=1, source_target_pairs={{0,2},{1,3},{2,0},{3,1},{4,6},{5,7},{6,4},{7,5},{8,10},{9,11},{10,... | collective-permute-start | bytes 196616 | tf_op jit(solution)/shard_map/ppermute | solution.py:450
  96.3 9.1 %collective-permute-start.20 = (f32[128,128]{1,0:T(8,128)}, f32[128,128]{1,0:T(8,128)S(1)}, u32[]{:S(2)}, u32[]{:S(2)}) collective-permute-start(f32[128,128]{1,0:T(8,128)} %add_add_fusion.1), channel_id=1, source_target_pairs={{0,3},{1,2},{2,1},{3,0},{4,7},{5,6},{6,5},{7,4},{8,11},{9,10},{10,... | collective-permute-start | bytes 196616 | tf_op jit(solution)/shard_map/ppermute | solution.py:450
  97.9 8.9 %collective-permute-start.18 = (f32[128,128]{1,0:T(8,128)}, f32[128,128]{1,0:T(8,128)S(1)}, u32[]{:S(2)}, u32[]{:S(2)}) collective-permute-start(f32[128,128]{1,0:T(8,128)} %add_add_fusion.1), channel_id=1, source_target_pairs={{0,1},{1,0},{2,3},{3,2},{4,5},{5,4},{6,7},{7,6},{8,9},{9,8},{10,11... | collective-permute-start | bytes 196616 | tf_op jit(solution)/shard_map/ppermute | solution.py:450
  97.9 68.1 %collective-permute-start.6 = (f32[2,128,1024]{2,1,0:T(8,128)}, f32[2,128,1024]{2,1,0:T(8,128)S(1)}, u32[]{:S(2)}, u32[]{:S(2)}) collective-permute-start(f32[2,128,1024]{2,1,0:T(8,128)} %get-tuple-element.21), channel_id=1, source_target_pairs={{0,4},{1,5},{2,6},{3,7},{4,8},{5,9},{6,10},{7,11},{8,12},{9,13},{1... | collective-permute-start | bytes 3145736 | tf_op jit(solution)/shard_map/ppermute | solution.py:583
  99.8 66.2 %collective-permute-start.7 = (f32[2,128,1024]{2,1,0:T(8,128)}, f32[2,128,1024]{2,1,0:T(8,128)S(1)}, u32[]{:S(2)}, u32[]{:S(2)}) collective-permute-start(f32[2,128,1024]{2,1,0:T(8,128)} %get-tuple-element.22), channel_id=1, source_target_pairs={{4,0},{5,1},{6,2},{7,3},{8,4},{9,5},{10,6},{11,7},{12,8},{13,9},{1... | collective-permute-start | bytes 3145736 | tf_op jit(solution)/shard_map/ppermute | solution.py:583
  101.1 0.6 copy-start.4
  101.8 64.3 %collective-permute-start.8 = (f32[2,1024,128]{2,1,0:T(8,128)}, f32[2,1024,128]{2,1,0:T(8,128)S(1)}, u32[]{:S(2)}, u32[]{:S(2)}) collective-permute-start(f32[2,1024,128]{2,1,0:T(8,128)} %get-tuple-element.23), channel_id=1, source_target_pairs={{0,1},{1,2},{2,3},{4,5},{5,6},{6,7},{8,9},{9,10},{10,11},{12,13},{... | collective-permute-start | bytes 3145736 | tf_op jit(solution)/shard_map/ppermute | solution.py:583
  105.5 1.3 copy-start.5
  105.5 60.6 %collective-permute-start.9 = (f32[2,1024,128]{2,1,0:T(8,128)}, f32[2,1024,128]{2,1,0:T(8,128)}, u32[]{:S(2)}, u32[]{:S(2)}) collective-permute-start(f32[2,1024,128]{2,1,0:T(8,128)} %get-tuple-element.24), channel_id=1, source_target_pairs={{1,0},{2,1},{3,2},{5,4},{6,5},{7,6},{9,8},{10,9},{11,10},{13,12},{... | collective-permute-start | bytes 3145736 | tf_op jit(solution)/shard_map/ppermute | solution.py:583
  106.8 0.6 copy-start.6
  107.4 1.7 collective-permute-start.11
  109.1 43.4 %copy-start = (f32[2,128,128]{2,1,0:T(8,128)}, f32[2,128,128]{2,1,0:T(8,128)S(1)}, u32[]{:S(2)}) copy-start(f32[2,128,128]{2,1,0:T(8,128)S(1)} %collective-permute-done.11.refs_5_) | copy-start | bytes 393220
  109.1 30.9 %collective-permute-start.21 = (f32[128,128]{1,0:T(8,128)S(1)}, f32[128,128]{1,0:T(8,128)S(1)}, u32[]{:S(2)}, u32[]{:S(2)}) collective-permute-start(f32[128,128]{1,0:T(8,128)S(1)} %get-tuple-element.32), channel_id=1, source_target_pairs={{0,8},{4,12},{8,16},{12,20},{16,24},{20,28},{24,0},{28,4},{1,9},{5... | collective-permute-start | bytes 196616 | tf_op jit(solution)/shard_map/ppermute | solution.py:429
  140.0 7.4 %collective-permute-start.22 = (f32[128,128]{1,0:T(8,128)S(1)}, f32[128,128]{1,0:T(8,128)S(1)}, u32[]{:S(2)}, u32[]{:S(2)}) collective-permute-start(f32[128,128]{1,0:T(8,128)S(1)} %get-tuple-element.32), channel_id=1, source_target_pairs={{0,16},{4,20},{8,24},{12,28},{16,0},{20,4},{24,8},{28,12},{1,17},{... | collective-permute-start | bytes 196616 | tf_op jit(solution)/shard_map/ppermute | solution.py:429
  147.5 4.3 %collective-permute-start.23 = (f32[128,128]{1,0:T(8,128)S(1)}, f32[128,128]{1,0:T(8,128)S(1)}, u32[]{:S(2)}, u32[]{:S(2)}) collective-permute-start(f32[128,128]{1,0:T(8,128)S(1)} %get-tuple-element.32), channel_id=1, source_target_pairs={{0,24},{4,28},{8,0},{12,4},{16,8},{20,12},{24,16},{28,20},{1,25},{... | collective-permute-start | bytes 196616 | tf_op jit(solution)/shard_map/ppermute | solution.py:429
  151.7 0.7 collective-permute-start.12
  152.5 0.7 copy-start.2
  153.1 5.7 %collective-permute-start.24 = (f32[512,128]{1,0:T(8,128)S(1)}, f32[512,128]{1,0:T(8,128)}, u32[]{:S(2)}, u32[]{:S(2)}) collective-permute-start(f32[512,128]{1,0:T(8,128)S(1)} %constant_dynamic-update-slice_fusion.refs_0_), channel_id=1, source_target_pairs={{0,4},{4,0},{8,12},{12,8},{16,20},{20,16},{24,28},{28,24},{1,5},{5... | collective-permute-start | bytes 786440 | tf_op jit(solution)/shard_map/ppermute | solution.py:429
  158.9 7.2 %collective-permute-start.13 = (f32[2,128,128]{2,1,0:T(8,128)}, f32[2,128,128]{2,1,0:T(8,128)S(1)}, u32[]{:S(2)}, u32[]{:S(2)}) collective-permute-start(f32[2,128,128]{2,1,0:T(8,128)} %get-tuple-element.28), channel_id=1, source_target_pairs={{5,0},{6,1},{7,2},{9,4},{10,5},{11,6},{13,8},{14,9},{15,10},{17,12... | collective-permute-start | bytes 393224 | tf_op jit(solution)/shard_map/ppermute | solution.py:583
  166.1 0.9 copy-start.1
  167.0 0.9 copy-start.3
